TPU v7x, 128 devices: a whole 4x4x4 slice. The times are simulated.
128 devices in a mesh: ctx: 8 (over y, x_lo), tp: 16 (over x_hi, z, core).
Axes of the slice: x: 4 (x_hi: 2, x_lo: 2; x = x_hi * 2 + x_lo), y: 4, z: 4, core: 2. Of those that a mesh axis runs over, the one named last changes fastest.
Arguments:
- hidden_input: bfloat16 [3072, 8192], P('ctx'), may hold values from -6 to 6
- output_cotangent: bfloat16 [3072, 8192], P('ctx', 'tp'), may hold values from -6 to 6
- query_projection: bfloat16 [8192, 4096], P(None, 'tp')
- key_value_projection: bfloat16 [8192, 2048], P(None, 'tp')
- output_projection: bfloat16 [4096, 8192], P('tp'), may hold values from -0.09375 to 0.09375
- adapter_qkv_down_store: bfloat16 [32, 8192, 192], P('ctx', 'tp'), may hold values from -0.0625 to 0.0625
- adapter_query_up: bfloat16 [32, 64, 4096], P('ctx', None, 'tp'), may hold values from -0.375 to 0.375
- adapter_key_value_up: bfloat16 [32, 64, 2048], P('ctx', None, 'tp'), may hold values from -0.375 to 0.375
- adapter_output_down: bfloat16 [32, 4096, 64], P('ctx', 'tp'), may hold values from -0.1875 to 0.1875
- adapter_output_up: bfloat16 [32, 64, 8192], P('ctx', None, 'tp'), may hold values from -0.75 to 0.75
- crop_token_length: int32 [4], replicated, may hold values from 1 to 2688, 3072 in all
- tenant_per_block: int32 [24], replicated, may hold values from 0 to 31, as said below
- tenant_store_row: int32 [32], replicated, may hold values from 0 to 31, as said below
Outputs:
- output: bfloat16 [3072, 8192], P('ctx', 'tp')
- hidden_input_gradient: bfloat16 [3072, 8192], P('ctx', 'tp')
- grad_down_qkv: float32 [32, 8192, 192], P('ctx', 'tp')
- grad_up_q: float32 [32, 64, 4096], P('ctx', None, 'tp')
- grad_up_kv: float32 [32, 64, 2048], P('ctx', None, 'tp')
- grad_down_o: float32 [32, 4096, 64], P('ctx', 'tp')
- grad_up_o: float32 [32, 64, 8192], P('ctx', None, 'tp')
Inputs may be any that keep to these rules, and one draw needn't show every extreme that they name: A permutation: tenant t's adapters are at store row tenant_store_row[t]; rows j * 4 to (j + 1) * 4 - 1 belong to owner j. `tenant_per_block`: of the 3 blocks of one index of ctx, at most 1 name tenants of one owner, and some owner is named that often.
All inputs are finite; a program needn't handle non-finite values.
Results may differ from a plain program's by a relative error of at most 0.038.
Values may be sent and summed in bfloat16 or wider, within the bound.
A program may use at most 128 MiB of HBM per device.

v0:
```python
import math

import jax
import jax.numpy as jnp
from jax import lax
from jax.sharding import PartitionSpec as P

HEAD_SIZE = 128
KEY_VALUE_HEADS = 8
ADAPTER_RANK = 64
BLK = 128
KBLK = 512


NEG = -1e30
ROPE_BASE = 1000000.0


def partner_2(value, axis, stride):
    mask = 2**stride
    pairs = [(source, source ^ mask) for source in range(lax.axis_size(axis))]
    return lax.ppermute(value, axis, pairs)


def rope_pair(positions):
    half_dim = HEAD_SIZE // 2
    exponent = jnp.arange(half_dim, dtype=jnp.float32) * (2.0 / HEAD_SIZE)
    frequency = jnp.exp(-exponent * math.log(ROPE_BASE))
    angles = positions.astype(jnp.float32)[:, None] * frequency[None, :]
    return (jnp.cos(angles), jnp.sin(angles))


def rotate(values, cosine, sine_tab):
    half_dim = values.shape[-1] // 2
    first_half = values[..., :half_dim]
    second = values[..., half_dim:]
    return jnp.concatenate(
        [first_half * cosine - second * sine_tab, second * cosine + first_half * sine_tab], axis=-1
    )


def rotate_back(gradient, cosine, sine_tab):
    half_dim = gradient.shape[-1] // 2
    first_half = gradient[..., :half_dim]
    second = gradient[..., half_dim:]
    return jnp.concatenate(
        [first_half * cosine + second * sine_tab, second * cosine - first_half * sine_tab], axis=-1
    )


def narrow_round(values):
    return lax.optimization_barrier(values.astype(jnp.bfloat16)).astype(jnp.float32)


def grouped_by_slot(slot_table, store_table):
    return jnp.einsum(
        "ics,s...->ic...", slot_table, store_table, preferred_element_type=jnp.float32
    ).astype(jnp.bfloat16)


def per_block(pick_narrow, fetched_one):
    return jnp.einsum(
        "boc,oc...->b...", pick_narrow, fetched_one, preferred_element_type=jnp.float32
    ).astype(jnp.bfloat16)


def body(
    hidden_input,
    output_cotangent,
    query_projection,
    key_value_projection,
    output_projection,
    adapter_qkv_down_store,
    adapter_query_up,
    adapter_key_value_up,
    adapter_output_down,
    adapter_output_up,
    crop_token_length,
    tenant_per_block,
    tenant_store_row,
):
    ctx_count = lax.axis_size("ctx")
    tp_count = lax.axis_size("tp")
    ctx_index = lax.axis_index("ctx")
    tp_index = lax.axis_index("tp")
    rows_dev = hidden_input.shape[0]
    tokens = rows_dev * ctx_count
    head_cols = query_projection.shape[1]
    local_heads = head_cols // HEAD_SIZE
    kv_cols = key_value_projection.shape[1]
    out_cols = output_cotangent.shape[1]
    width_slice = adapter_qkv_down_store.shape[1]
    tenant_owner = adapter_qkv_down_store.shape[0]
    blocks_dev = rows_dev // BLK
    per_owner = (blocks_dev + ctx_count - 1) // ctx_count
    pair_bits = (tp_count // KEY_VALUE_HEADS).bit_length() - 1
    score_scale = HEAD_SIZE ** (-0.5)
    tenant_ids = jnp.arange(tenant_store_row.shape[0], dtype=jnp.int32)
    rows_per_block = jnp.sum(
        jnp.where(tenant_per_block[:, None] == tenant_ids[None, :], tenant_store_row[None, :], 0),
        axis=1,
    )
    shard_rows = rows_per_block.reshape(ctx_count, blocks_dev)
    shard_owner = shard_rows // tenant_owner
    block_ids = jnp.arange(blocks_dev, dtype=jnp.int32)
    earlier = (shard_owner[:, :, None] == shard_owner[:, None, :]) & (
        block_ids[None, None, :] < block_ids[None, :, None]
    )
    shard_rank = jnp.sum(earlier.astype(jnp.int32), axis=2)
    slot_ids = jnp.arange(per_owner, dtype=jnp.int32)
    store_ids = jnp.arange(tenant_owner, dtype=jnp.int32)
    owner_ids = jnp.arange(ctx_count, dtype=jnp.int32)
    served = (
        (shard_owner == ctx_index)[:, :, None, None]
        & (shard_rank[:, :, None, None] == slot_ids[None, None, :, None])
        & (
            (shard_rows - ctx_index * tenant_owner)[:, :, None, None]
            == store_ids[None, None, None, :]
        )
    )
    serve_table = jnp.sum(served.astype(jnp.float32), axis=1)
    serve_reduced_width = serve_table.astype(jnp.bfloat16)
    my_owner = lax.dynamic_index_in_dim(shard_owner, ctx_index, 0, keepdims=False)
    my_rank = lax.dynamic_index_in_dim(shard_rank, ctx_index, 0, keepdims=False)
    pick_table = (
        (my_owner[:, None, None] == owner_ids[None, :, None])
        & (my_rank[:, None, None] == slot_ids[None, None, :])
    ).astype(jnp.float32)
    pick_narrow = pick_table.astype(jnp.bfloat16)
    fetched = (
        lax.all_to_all(
            grouped_by_slot(serve_reduced_width, adapter_qkv_down_store),
            "ctx",
            split_axis=0,
            concat_axis=0,
            tiled=True,
        ),
        lax.all_to_all(
            grouped_by_slot(serve_reduced_width, adapter_query_up),
            "ctx",
            split_axis=0,
            concat_axis=0,
            tiled=True,
        ),
        lax.all_to_all(
            grouped_by_slot(serve_reduced_width, adapter_key_value_up),
            "ctx",
            split_axis=0,
            concat_axis=0,
            tiled=True,
        ),
        lax.all_to_all(
            grouped_by_slot(serve_reduced_width, adapter_output_down),
            "ctx",
            split_axis=0,
            concat_axis=0,
            tiled=True,
        ),
        lax.all_to_all(
            grouped_by_slot(serve_reduced_width, adapter_output_up),
            "ctx",
            split_axis=0,
            concat_axis=0,
            tiled=True,
        ),
    )
    query_key_value_down = per_block(pick_narrow, fetched[0])
    query_up_map = per_block(pick_narrow, fetched[1])
    key_value_up_map = per_block(pick_narrow, fetched[2])
    output_down_map = per_block(pick_narrow, fetched[3])
    output_up_map = per_block(pick_narrow, fetched[4])
    input_slice = lax.dynamic_slice_in_dim(
        hidden_input, tp_index * width_slice, width_slice, 1
    ).reshape(blocks_dev, BLK, width_slice)
    grad_blocks = output_cotangent.reshape(blocks_dev, BLK, out_cols)
    lowrank_portion = jnp.einsum(
        "uaj,ujx->uax", input_slice, query_key_value_down, preferred_element_type=jnp.float32
    )
    out_part = jnp.einsum(
        "bkc,brc->bkr", grad_blocks, output_up_map, preferred_element_type=jnp.float32
    )
    low_sum, out_sum = lax.psum((lowrank_portion, out_part), "tp")
    low_in = low_sum.astype(jnp.bfloat16)
    low_grad_o = out_sum.astype(jnp.bfloat16)
    low_q = low_in[..., :ADAPTER_RANK]
    low_k = low_in[..., ADAPTER_RANK : 2 * ADAPTER_RANK]
    low_v = low_in[..., 2 * ADAPTER_RANK :]
    my_pos = ctx_index * rows_dev + jnp.arange(rows_dev, dtype=jnp.int32)
    cosine, sine_tab = rope_pair(my_pos)
    query_lin = jnp.dot(
        hidden_input, query_projection, preferred_element_type=jnp.float32
    ) + jnp.einsum("pto,pon->ptn", low_q, query_up_map, preferred_element_type=jnp.float32).reshape(
        rows_dev, head_cols
    )
    query_rot = rotate(
        query_lin.reshape(rows_dev, local_heads, HEAD_SIZE),
        cosine[:, None, :],
        sine_tab[:, None, :],
    ).astype(jnp.bfloat16)
    kv_index = tp_index * kv_cols + jnp.arange(kv_cols, dtype=jnp.int32)
    is_value = kv_index // HEAD_SIZE % 2 == 1
    kv_low = jnp.where(
        is_value,
        jnp.einsum("pto,pon->ptn", low_v, key_value_up_map, preferred_element_type=jnp.float32),
        jnp.einsum("pto,pon->ptn", low_k, key_value_up_map, preferred_element_type=jnp.float32),
    ).reshape(rows_dev, kv_cols)
    kv_local = (
        jnp.dot(hidden_input, key_value_projection, preferred_element_type=jnp.float32) + kv_low
    ).astype(jnp.bfloat16)
    bit_no = 0
    partner = partner_2(kv_local, "tp", bit_no)
    is_lower = tp_index // (1 << bit_no) % 2 == 0
    kv_local = jnp.where(
        is_lower,
        jnp.concatenate([kv_local, partner], axis=1),
        jnp.concatenate([partner, kv_local], axis=1),
    )
    key_rot = rotate(kv_local[:, :HEAD_SIZE].astype(jnp.float32), cosine, sine_tab).astype(
        jnp.bfloat16
    )
    kv_rot = jnp.concatenate([key_rot, kv_local[:, HEAD_SIZE:]], axis=1)
    kv_all = lax.all_gather(kv_rot, "ctx", axis=0, tiled=True)
    crop_ends = jnp.cumsum(crop_token_length)

    def segment_of(positions):
        return jnp.sum((positions[:, None] >= crop_ends[None, :]).astype(jnp.int32), axis=1)

    all_pos = jnp.arange(tokens, dtype=jnp.int32)
    key_seg = segment_of(all_pos)
    row_count = local_heads * rows_dev
    query_rows = query_rot.transpose(1, 0, 2).reshape(row_count, HEAD_SIZE)
    row_pos = jnp.tile(my_pos, local_heads)
    row_seg = jnp.tile(segment_of(my_pos), local_heads)
    block_list = jnp.arange(tokens // KBLK, dtype=jnp.int32)

    def key_block(block_no):
        start_at = block_no * KBLK
        kv_block = lax.dynamic_slice_in_dim(kv_all, start_at, KBLK, 0)
        key_pos = start_at + jnp.arange(KBLK, dtype=jnp.int32)
        seg_block = lax.dynamic_slice_in_dim(key_seg, start_at, KBLK, 0)
        allowed = (key_pos[None, :] <= row_pos[:, None]) & (seg_block[None, :] == row_seg[:, None])
        return (kv_block[:, :HEAD_SIZE], kv_block[:, HEAD_SIZE:], allowed)

    def masked_scores(key_rows, allowed):
        raw_scores = (
            jnp.einsum("qd,kd->qk", query_rows, key_rows, preferred_element_type=jnp.float32)
            * score_scale
        )
        return jnp.where(allowed, raw_scores, NEG)

    def stats_step(running, block_no):
        key_rows, value_rows, allowed = key_block(block_no)
        scores = masked_scores(key_rows, allowed)
        new_max = jnp.maximum(running[0], jnp.max(scores, axis=1))
        new_sum = running[1] * jnp.exp(running[0] - new_max) + jnp.sum(
            jnp.exp(scores - new_max[:, None]), axis=1
        )
        running = (new_max, new_sum)
        return (running, None)

    start_stats = (jnp.full((row_count,), NEG, jnp.float32), jnp.zeros((row_count,), jnp.float32))
    stats, unused = lax.scan(stats_step, start_stats, block_list)
    log_norm = stats[0] + jnp.log(stats[1])

    def output_step(running, block_no):
        key_rows, value_rows, allowed = key_block(block_no)
        weights = jnp.exp(masked_scores(key_rows, allowed) - log_norm[:, None]).astype(jnp.bfloat16)
        running = running + jnp.dot(weights, value_rows, preferred_element_type=jnp.float32)
        return (running, None)

    attended, unused = lax.scan(
        output_step, jnp.zeros((row_count, HEAD_SIZE), jnp.float32), block_list
    )
    out_rows = attended.astype(jnp.bfloat16)
    attn_out = (
        out_rows.reshape(local_heads, rows_dev, HEAD_SIZE)
        .transpose(1, 0, 2)
        .reshape(rows_dev, head_cols)
    )
    out_blocks = attn_out.reshape(blocks_dev, BLK, head_cols)
    lowrank_output = lax.psum(
        jnp.einsum(
            "bkc,bcr->bkr", out_blocks, output_down_map, preferred_element_type=jnp.float32
        ).astype(jnp.bfloat16),
        "tp",
    )
    adapter_result = jnp.einsum(
        "pto,pon->ptn", lowrank_output, output_up_map, preferred_element_type=jnp.float32
    ).reshape(rows_dev, out_cols)
    heads_total_sum = lax.psum_scatter(
        jnp.dot(attn_out, output_projection, preferred_element_type=jnp.float32).astype(
            jnp.bfloat16
        ),
        "tp",
        scatter_dimension=1,
        tiled=True,
    ).astype(jnp.float32)
    output = (heads_total_sum + adapter_result).astype(jnp.bfloat16)
    adapter_output_delta = jnp.einsum(
        "bkr,bcr->bkc", low_grad_o, output_down_map, preferred_element_type=jnp.float32
    ).reshape(rows_dev, head_cols)
    pieces = lax.all_gather(output_cotangent, "tp", axis=1, tiled=True)
    groups = pieces.shape[1] // out_cols
    group_terms = jnp.einsum(
        "sgc,hgc->gsh",
        pieces.reshape(rows_dev, groups, out_cols),
        output_projection.reshape(head_cols, groups, out_cols),
        preferred_element_type=jnp.float32,
    )
    head_gradient = jnp.sum(narrow_round(group_terms), axis=0)
    attention_gradient = (head_gradient + adapter_output_delta).astype(jnp.bfloat16)
    grad_rows = (
        attention_gradient.reshape(rows_dev, local_heads, HEAD_SIZE)
        .transpose(1, 0, 2)
        .reshape(row_count, HEAD_SIZE)
    )
    row_delta = jnp.sum(grad_rows.astype(jnp.float32) * out_rows.astype(jnp.float32), axis=1)

    def grad_step(running, block_no):
        key_rows, value_rows, allowed = key_block(block_no)
        weights = jnp.exp(masked_scores(key_rows, allowed) - log_norm[:, None])
        weights_narrow = weights.astype(jnp.bfloat16)
        grad_weights = jnp.einsum(
            "qd,kd->qk", grad_rows, value_rows, preferred_element_type=jnp.float32
        )
        grad_scores = (weights * (grad_weights - row_delta[:, None])).astype(jnp.bfloat16)
        new_acc = running + jnp.dot(grad_scores, key_rows, preferred_element_type=jnp.float32)
        key_grad = (
            jnp.einsum("qk,qd->kd", grad_scores, query_rows, preferred_element_type=jnp.float32)
            * score_scale
        )
        value_grad = jnp.einsum(
            "qk,qd->kd", weights_narrow, grad_rows, preferred_element_type=jnp.float32
        )
        return (new_acc, jnp.concatenate([key_grad, value_grad], axis=1))

    query_acc, kv_blocks = lax.scan(
        grad_step, jnp.zeros((row_count, HEAD_SIZE), jnp.float32), block_list
    )
    grad_query = (
        (query_acc * score_scale).reshape(local_heads, rows_dev, HEAD_SIZE).transpose(1, 0, 2)
    )
    grad_q = (
        rotate_back(grad_query, cosine[:, None, :], sine_tab[:, None, :])
        .reshape(rows_dev, head_cols)
        .astype(jnp.bfloat16)
    )
    all_cos, all_sin = rope_pair(all_pos)
    kv_partial = kv_blocks.reshape(tokens, 2 * HEAD_SIZE)
    kv_partial = jnp.concatenate(
        [rotate_back(kv_partial[:, :HEAD_SIZE], all_cos, all_sin), kv_partial[:, HEAD_SIZE:]],
        axis=1,
    )
    reduced = lax.psum_scatter(
        kv_partial.astype(jnp.bfloat16), "ctx", scatter_dimension=0, tiled=True
    ).astype(jnp.float32)
    for bit_no in reversed(range(pair_bits)):
        half_cols = reduced.shape[1] // 2
        is_lower = tp_index // (1 << bit_no) % 2 == 0
        keep_part = jnp.where(is_lower, reduced[:, :half_cols], reduced[:, half_cols:])
        send_part = jnp.where(is_lower, reduced[:, half_cols:], reduced[:, :half_cols])
        reduced = keep_part + partner_2(send_part.astype(jnp.bfloat16), "tp", bit_no).astype(
            send_part.dtype
        )
    grad_kv = reduced.astype(jnp.bfloat16)
    grad_q_blocks = grad_q.reshape(blocks_dev, BLK, head_cols)
    grad_kv_blocks = grad_kv.reshape(blocks_dev, BLK, kv_cols)
    zero_narrow = jnp.zeros((), jnp.bfloat16)
    key_part = jnp.where(is_value, zero_narrow, grad_kv_blocks)
    value_part = jnp.where(is_value, grad_kv_blocks, zero_narrow)
    low_grad_part = jnp.concatenate(
        [
            jnp.einsum(
                "bkc,brc->bkr", grad_q_blocks, query_up_map, preferred_element_type=jnp.float32
            ),
            jnp.einsum(
                "bkc,brc->bkr", key_part, key_value_up_map, preferred_element_type=jnp.float32
            ),
            jnp.einsum(
                "bkc,brc->bkr", value_part, key_value_up_map, preferred_element_type=jnp.float32
            ),
        ],
        axis=2,
    )
    lowrank_gradient = lax.psum(low_grad_part.astype(jnp.bfloat16), "tp")
    input_part = jnp.einsum(
        "sc,dc->sd", grad_q, query_projection, preferred_element_type=jnp.float32
    ) + jnp.einsum("sc,dc->sd", grad_kv, key_value_projection, preferred_element_type=jnp.float32)
    input_total_sum = lax.psum_scatter(
        input_part.astype(jnp.bfloat16), "tp", scatter_dimension=1, tiled=True
    ).astype(jnp.float32)
    adapter_input_delta = jnp.einsum(
        "fcn,fjn->fcj", lowrank_gradient, query_key_value_down, preferred_element_type=jnp.float32
    ).reshape(rows_dev, width_slice)
    hidden_input_gradient = (input_total_sum + adapter_input_delta).astype(jnp.bfloat16)
    block_down_qkv = jnp.einsum(
        "wov,woe->wve", input_slice, lowrank_gradient, preferred_element_type=jnp.float32
    )
    block_up_q = jnp.einsum(
        "bkr,bkc->brc", low_q, grad_q_blocks, preferred_element_type=jnp.float32
    )
    block_up_kv = jnp.where(
        is_value,
        jnp.einsum("bkr,bkc->brc", low_v, grad_kv_blocks, preferred_element_type=jnp.float32),
        jnp.einsum("bkr,bkc->brc", low_k, grad_kv_blocks, preferred_element_type=jnp.float32),
    )
    block_down_o = jnp.einsum(
        "bkc,bkr->bcr", out_blocks, low_grad_o, preferred_element_type=jnp.float32
    )
    block_up_o = jnp.einsum(
        "bkr,bkc->brc", lowrank_output, grad_blocks, preferred_element_type=jnp.float32
    )

    def to_owner(block_grad):
        return jnp.einsum(
            "boc,b...->oc...", pick_table, block_grad, precision=lax.Precision.HIGHEST
        )

    def to_store(arrived):
        return jnp.einsum("ics,ic...->s...", serve_table, arrived, precision=lax.Precision.HIGHEST)

    returned = (
        lax.all_to_all(
            to_owner(block_down_qkv).astype(jnp.bfloat16),
            "ctx",
            split_axis=0,
            concat_axis=0,
            tiled=True,
        ).astype(jnp.float32),
        lax.all_to_all(
            to_owner(block_up_q).astype(jnp.bfloat16),
            "ctx",
            split_axis=0,
            concat_axis=0,
            tiled=True,
        ).astype(jnp.float32),
        lax.all_to_all(
            to_owner(block_up_kv).astype(jnp.bfloat16),
            "ctx",
            split_axis=0,
            concat_axis=0,
            tiled=True,
        ).astype(jnp.float32),
        lax.all_to_all(
            to_owner(block_down_o).astype(jnp.bfloat16),
            "ctx",
            split_axis=0,
            concat_axis=0,
            tiled=True,
        ).astype(jnp.float32),
        lax.all_to_all(
            to_owner(block_up_o).astype(jnp.bfloat16),
            "ctx",
            split_axis=0,
            concat_axis=0,
            tiled=True,
        ).astype(jnp.float32),
    )
    return (
        output,
        hidden_input_gradient,
        to_store(returned[0]),
        to_store(returned[1]),
        to_store(returned[2]),
        to_store(returned[3]),
        to_store(returned[4]),
    )


def solution(mesh):
    in_specs = (
        P("ctx", None),
        P("ctx", "tp"),
        P(None, "tp"),
        P(None, "tp"),
        P("tp", None),
        P("ctx", "tp", None),
        P("ctx", None, "tp"),
        P("ctx", None, "tp"),
        P("ctx", "tp", None),
        P("ctx", None, "tp"),
        P(),
        P(),
        P(),
    )
    out_specs = (
        P("ctx", "tp"),
        P("ctx", "tp"),
        P("ctx", "tp", None),
        P("ctx", None, "tp"),
        P("ctx", None, "tp"),
        P("ctx", "tp", None),
        P("ctx", None, "tp"),
    )
    return jax.shard_map(body, mesh=mesh, in_specs=in_specs, out_specs=out_specs, check_vma=False)
```

profile of v0, /device:TPU:0, one launch (start us, length us, event | category | flops | bytes accessed | tf_op | source)
XLA Modules:
  0.0 721.1 jit_solution(13131497351691518213)
XLA Ops:
  10.9 5.6 all-to-all-start.1
  18.8 4.4 all-to-all-done.1
  29.2 6.5 all-to-all-done.4
  35.7 4.3 all-to-all-start
  44.9 14.1 %all-to-all-done = bf16[8,1,512,192]{2,3,1,0:T(8,128)(2,1)} async-done(((bf16[8,1,512,192]{2,3,1,0:T(8,128)(2,1)}), bf16[8,1,512,192]{2,3,1,0:T(8,128)(2,1)}, u32[]{:S(2)}, u32[]{:S(2)}) %all-to-all-start) | async-done | bytes 1572896 | tf_op jit(solution)/shard_map/all_to_all | solution.py:131
  62.8 71.0 %all-reduce.5 = (bf16[3,128,192]{1,2,0:T(8,128)(2,1)S(1)}, bf16[3,128,64]{1,2,0:T(8,128)(2,1)}) all-reduce(f32[3,128,192]{1,2,0:T(8,128)S(1)} %fusion.131, f32[3,128,64]{1,2,0:T(8,128)S(1)} %convolution_bitcast_fusion), channel_id=1, replica_groups=mesh['ctx'=8,'tp'=16] {'tp'}, use_global_device_ids=true, to_apply=%region_3.4 | all-reduce | flops 98304 | bytes 589824 | tf_op jit(solution)/shard_map/psum | solution.py:182
  134.4 4.7 fusion.67
  143.8 4.1 all-to-all-start.3
  150.6 8.4 %all-to-all-done.3 = bf16[8,1,256,64]{2,3,1,0:T(8,128)(2,1)S(1)} async-done(((bf16[8,1,256,64]{2,3,1,0:T(8,128)(2,1)}), bf16[8,1,256,64]{2,3,1,0:T(8,128)(2,1)S(1)}, u32[]{:S(2)}, u32[]{:S(2)}) %all-to-all-start.3) | async-done | bytes 262176 | tf_op jit(solution)/shard_map/all_to_all | solution.py:152
  163.0 10.2 %all-to-all-done.2 = bf16[8,1,64,256]{3,2,1,0:T(8,128)(2,1)S(1)} async-done(((bf16[8,1,64,256]{3,2,1,0:T(8,128)(2,1)}), bf16[8,1,64,256]{3,2,1,0:T(8,128)(2,1)S(1)}, u32[]{:S(2)}, u32[]{:S(2)}) %all-to-all-start.2) | async-done | bytes 262176 | tf_op jit(solution)/shard_map/all_to_all | solution.py:138
  175.1 6.6 convolution_add_fusion.1
  182.0 5.9 all-gather.3.cloned.1.call-done
  190.4 37.8 %while.37 = (s32[]{:T(128)}, f32[768]{0:T(1024)S(1)}, f32[768]{0:T(1024)S(1)}, s32[6]{0:T(128)S(1)}, s32[3072]{0:T(1024)}, /*index=5*/bf16[3072,256]{1,0:T(8,128...) while((s32[]{:T(128)}, f32[768]{0:T(1024)S(1)}, ...), condition=%wide.region_10.11_spmd.clone, body=%wide.region_7.10_spmd.clone.sunk | while | flops 103813384 | bytes 3551446 | solution.py:262
  228.8 24.7 %while.38 = (s32[]{:T(128)}, f32[768,128]{1,0:T(8,128)S(1)}, s32[6]{0:T(128)S(1)}, s32[3072]{0:T(1024)}, bf16[3072,256]{1,0:T(8,128)(2,1)}, /*index=5*/bf16[768,...) while((s32[]{:T(128)}, f32[768,128]{1,0:T(8,128)S(1)}, ...), condition=%wide.region_12.13_spmd.clone, body=%wide.region_11.12_spmd.clone.sunk | while | flops 204276224 | bytes 1289444 | solution.py:271
  254.2 6.0 fusion.47
  262.6 64.9 %while.39 = (s32[]{:T(128)}, f32[768,128]{1,0:T(8,128)}, f32[6,512,256]{2,1,0:T(8,128)}, s32[6]{0:T(128)S(1)}, s32[3072]{0:T(1024)}, /*index=5*/bf16[3072,256]{1...) while((s32[]{:T(128)}, f32[768,128]{1,0:T(8,128)}, ...), condition=%wide.region_19.20_spmd.clone, body=%wide.region_18.19_spmd.clone.sunk | while | flops 507642368 | bytes 19050796 | solution.py:337
  329.8 4.1 fusion.169
  338.5 5.0 fusion.75
  351.9 39.6 %reduce-scatter.6.cloned.1.call-done = bf16[384,256]{1,0:T(8,128)(2,1)} async-done(((bf16[3072,256]{1,0:T(8,128)(2,1)}), bf16[384,256]{1,0:T(8,128)(2,1)}) %reduce-scatter.6.cloned.1.call-update) | async-done | bytes 196624 | tf_op jit(solution)/shard_map/reduce_scatter | solution.py:354
  396.3 6.7 convolution_convert_fusion
  403.1 4.1 fusion.174
  407.2 4.5 add_convert_fusion
  419.0 69.5 %psum.29 = bf16[3,128,64]{1,2,0:T(8,128)(2,1)S(1)} all-reduce(bf16[3,128,64]{1,2,0:T(8,128)(2,1)S(1)} %convolution_convert_fusion.14), channel_id=1, replica_groups=mesh['ctx'=8,'tp'=16] {'tp'}, use_global_device_ids=true, to_apply=%region_14.15 | all-reduce | flops 24576 | bytes 98304 | tf_op jit(solution)/shard_map/psum | solution.py:281
  492.8 4.8 all-to-all-start.8
  497.8 7.2 all-to-all-done.8
  505.0 4.1 all-to-all-start.9
  510.3 14.6 %all-reduce.4.cloned.1.call-done = bf16[3,128,192]{1,2,0:T(8,128)(2,1)} async-done(((bf16[3,128,192]{1,2,0:T(8,128)(2,1)}), bf16[3,128,192]{1,2,0:T(8,128)(2,1)}) %all-reduce.4.cloned.1.call-update) | async-done | bytes 147472 | tf_op jit(solution)/shard_map/psum | solution.py:385
  526.3 5.6 all-to-all-start.7
  538.6 4.3 all-to-all-start.5
  551.5 10.9 %all-to-all-done.5 = bf16[8,1,512,192]{2,3,1,0:T(8,128)(2,1)} async-done(((bf16[8,1,512,192]{2,3,1,0:T(8,128)(2,1)}), bf16[8,1,512,192]{2,3,1,0:T(8,128)(2,1)}, u32[]{:S(2)}, u32[]{:S(2)}) %all-to-all-start.5) | async-done | bytes 1572896 | tf_op jit(solution)/shard_map/all_to_all | solution.py:423
  567.4 51.5 %reduce-scatter.4.cloned.1.call-done = bf16[384,512]{1,0:T(8,128)(2,1)} async-done(((bf16[384,8192]{1,0:T(8,128)(2,1)}), bf16[384,512]{1,0:T(8,128)(2,1)}) %reduce-scatter.4.cloned.1.call-update) | async-done | bytes 393232 | tf_op jit(solution)/shard_map/reduce_scatter | solution.py:290
  620.8 90.9 %reduce-scatter.8.cloned.1.call-done = bf16[384,512]{1,0:T(8,128)(2,1)} async-done(((bf16[384,8192]{1,0:T(8,128)(2,1)}), bf16[384,512]{1,0:T(8,128)(2,1)}) %reduce-scatter.8.cloned.1.call-update) | async-done | bytes 393232 | tf_op jit(solution)/shard_map/reduce_scatter | solution.py:389
  (456 shorter events, 213.6 us)
Async XLA Ops:
  7.2 127.2 %copy-start = (bf16[8192,128]{1,0:T(8,128)(2,1)S(1)}, bf16[8192,128]{1,0:T(8,128)(2,1)}, u32[]{:S(2)}) copy-start(bf16[8192,128]{1,0:T(8,128)(2,1)} %param.22) | copy-start | bytes 6291460
  10.9 12.3 %all-to-all-start.1 = ((bf16[8,1,64,128]{3,2,1,0:T(8,128)(2,1)}), bf16[8,1,64,128]{3,2,1,0:T(8,128)(2,1)S(1)}, u32[]{:S(2)}, u32[]{:S(2)}) async-start(bf16[8,1,64,128]{3,2,1,0:T(8,128)(2,1)} %copy.337), calls=%async_computation.1 | async-start | bytes 262144 | tf_op jit(solution)/shard_map/all_to_all | solution.py:145
  23.3 12.4 %all-to-all-start.4 = ((bf16[8,1,64,512]{3,2,1,0:T(8,128)(2,1)}), bf16[8,1,64,512]{3,2,1,0:T(8,128)(2,1)S(1)}, u32[]{:S(2)}, u32[]{:S(2)}) async-start(bf16[8,1,64,512]{3,2,1,0:T(8,128)(2,1)} %copy.356), calls=%async_computation.5 | async-start | bytes 1048576 | tf_op jit(solution)/shard_map/all_to_all | solution.py:159
  35.7 23.4 %all-to-all-start = ((bf16[8,1,512,192]{2,3,1,0:T(8,128)(2,1)}), bf16[8,1,512,192]{2,3,1,0:T(8,128)(2,1)}, u32[]{:S(2)}, u32[]{:S(2)}) async-start(bf16[8,1,512,192]{2,3,1,0:T(8,128)(2,1)} %copy.333), calls=%async_computation | async-start | bytes 3145728 | tf_op jit(solution)/shard_map/all_to_all | solution.py:131
  40.0 147.9 %all-gather.3.cloned.1.call-start = ((), (), s32[]{:S(2)}) async-start(), calls=%async_computation.13 | async-start | bytes 1769472 | tf_op jit(solution)/shard_map/all_gather | solution.py:222
  40.9 93.1 %copy-start.40 = (pred[128]{0:T(512)(128)(4,1)}, pred[128]{0:T(512)(128)(4,1)S(1)}, u32[]{:S(2)}) copy-start(pred[128]{0:T(512)(128)(4,1)S(1)} %fusion.159) | copy-start | bytes 388
  44.9 88.8 %copy-start.26 = (bf16[3,64,128]{2,0,1:T(4,128)(2,1)S(1)}, bf16[3,64,128]{2,0,1:T(4,128)(2,1)}, u32[]{:S(2)}) copy-start(bf16[3,64,128]{2,0,1:T(4,128)(2,1)} %fusion.106) | copy-start | bytes 147460
  133.8 40.2 %copy-start.22 = (bf16[3,128,192]{1,2,0:T(8,128)(2,1)}, bf16[3,128,192]{1,2,0:T(8,128)(2,1)S(1)}, u32[]{:S(2)}) copy-start(bf16[3,128,192]{1,2,0:T(8,128)(2,1)S(1)} %get-tuple-element.606) | copy-start | bytes 442372
  139.1 1.4 collective-permute-start
  141.0 40.7 %copy-start.13 = (f32[384,64]{0,1:T(8,128)}, f32[384,64]{0,1:T(8,128)S(1)}, u32[]{:S(2)}) copy-start(f32[384,64]{0,1:T(8,128)S(1)} %get-tuple-element.624) | copy-start | bytes 294916
  141.0 40.7 %copy-start.15 = (f32[384,64]{0,1:T(8,128)}, f32[384,64]{0,1:T(8,128)S(1)}, u32[]{:S(2)}) copy-start(f32[384,64]{0,1:T(8,128)S(1)} %get-tuple-element.625) | copy-start | bytes 294916
  141.8 111.7 %all-gather.5.cloned.1.call-start = ((), (), s32[]{:S(2)}) async-start(), calls=%async_computation.15 | async-start | bytes 6684672 | tf_op jit(solution)/shard_map/all_gather | solution.py:302
  142.8 19.9 %copy-start.37 = (pred[3,8]{1,0:T(4,128)(4,1)S(1)}, pred[3,8]{1,0:T(4,128)(4,1)}, u32[]{:S(2)}) copy-start(pred[3,8]{1,0:T(4,128)(4,1)} %copy-done.36) | copy-start | bytes 76
  143.1 30.4 %copy-start.31 = (bf16[3,128,64]{1,2,0:T(8,128)(2,1)S(1)}, bf16[3,128,64]{1,2,0:T(8,128)(2,1)}, u32[]{:S(2)}) copy-start(bf16[3,128,64]{1,2,0:T(8,128)(2,1)} %get-tuple-element.607) | copy-start | bytes 147460
  143.8 15.2 %all-to-all-start.3 = ((bf16[8,1,256,64]{2,3,1,0:T(8,128)(2,1)}), bf16[8,1,256,64]{2,3,1,0:T(8,128)(2,1)S(1)}, u32[]{:S(2)}, u32[]{:S(2)}) async-start(bf16[8,1,256,64]{2,3,1,0:T(8,128)(2,1)} %copy.352), calls=%async_computation.4 | async-start | bytes 524288 | tf_op jit(solution)/shard_map/all_to_all | solution.py:152
  159.0 14.1 %all-to-all-start.2 = ((bf16[8,1,64,256]{3,2,1,0:T(8,128)(2,1)}), bf16[8,1,64,256]{3,2,1,0:T(8,128)(2,1)S(1)}, u32[]{:S(2)}, u32[]{:S(2)}) async-start(bf16[8,1,64,256]{3,2,1,0:T(8,128)(2,1)} %copy.342), calls=%async_computation.2 | async-start | bytes 524288 | tf_op jit(solution)/shard_map/all_to_all | solution.py:138
  162.5 229.1 %reduce-scatter.6.cloned.1.call-start = ((), (), s32[]{:S(2)}) async-start(), calls=%async_computation.16 | async-start | bytes 1769472 | tf_op jit(solution)/shard_map/reduce_scatter | solution.py:354
  190.4 38.4 %copy-start.28 = (f32[768,128]{1,0:T(8,128)S(1)}, f32[768,128]{1,0:T(8,128)}, u32[]{:S(2)}) copy-start(f32[768,128]{1,0:T(8,128)} %custom-call.2) | copy-start | bytes 1179652
  350.2 174.7 %all-reduce.4.cloned.1.call-start = ((), (), s32[]{:S(2)}) async-start(), calls=%async_computation.18 | async-start | bytes 294912 | tf_op jit(solution)/shard_map/psum | solution.py:385
  351.5 41.2 %copy-start.19 = (bf16[3,64,256]{2,0,1:T(4,128)(2,1)S(1)}, bf16[3,64,256]{2,0,1:T(4,128)(2,1)}, u32[]{:S(2)}) copy-start(bf16[3,64,256]{2,0,1:T(4,128)(2,1)} %copy-done.18) | copy-start | bytes 294916
  351.5 41.3 %copy-start.8 = (bf16[768,128]{1,0:T(8,128)(2,1)S(1)}, bf16[768,128]{1,0:T(8,128)(2,1)}, u32[]{:S(2)}) copy-start(bf16[768,128]{1,0:T(8,128)(2,1)} %get-tuple-element.609) | copy-start | bytes 589828
  351.6 43.4 %copy-start.27 = (bf16[3,64,128]{2,0,1:T(4,128)(2,1)S(1)}, bf16[3,64,128]{2,0,1:T(4,128)(2,1)}, u32[]{:S(2)}) copy-start(bf16[3,64,128]{2,0,1:T(4,128)(2,1)} %fusion.106) | copy-start | bytes 147460
  351.6 43.4 %copy-start.41 = (pred[128]{0:T(512)(128)(4,1)S(1)}, pred[128]{0:T(512)(128)(4,1)}, u32[]{:S(2)}) copy-start(pred[128]{0:T(512)(128)(4,1)} %copy-done.40) | copy-start | bytes 388
  392.5 1.5 collective-permute-start.1
  396.1 222.9 %reduce-scatter.4.cloned.1.call-start = ((), (), s32[]{:S(2)}) async-start(), calls=%async_computation.14 | async-start | bytes 6684672 | tf_op jit(solution)/shard_map/reduce_scatter | solution.py:290
  403.0 308.7 %reduce-scatter.8.cloned.1.call-start = ((), (), s32[]{:S(2)}) async-start(), calls=%async_computation.17 | async-start | bytes 6684672 | tf_op jit(solution)/shard_map/reduce_scatter | solution.py:389
  411.9 77.6 %copy-start.5 = (bf16[384,512]{1,0:T(8,128)(2,1)S(1)}, bf16[384,512]{1,0:T(8,128)(2,1)}, u32[]{:S(2)}) copy-start(bf16[384,512]{1,0:T(8,128)(2,1)} %param.20) | copy-start | bytes 1179652
  414.3 78.6 %all-to-all-start.6 = ((bf16[8,1,64,256]{3,2,1,0:T(8,128)(2,1)}), bf16[8,1,64,256]{3,2,1,0:T(8,128)(2,1)S(1)}, u32[]{:S(2)}, u32[]{:S(2)}) async-start(bf16[8,1,64,256]{3,2,1,0:T(8,128)(2,1)} %copy.375), calls=%async_computation.9 | async-start | bytes 524288 | tf_op jit(solution)/shard_map/all_to_all | solution.py:430
  492.8 12.1 %all-to-all-start.8 = ((bf16[8,1,256,64]{2,3,1,0:T(8,128)(2,1)}), bf16[8,1,256,64]{2,3,1,0:T(8,128)(2,1)S(1)}, u32[]{:S(2)}, u32[]{:S(2)}) async-start(bf16[8,1,256,64]{2,3,1,0:T(8,128)(2,1)} %copy.381), calls=%async_computation.11 | async-start | bytes 524288 | tf_op jit(solution)/shard_map/all_to_all | solution.py:444
  505.0 21.3 %all-to-all-start.9 = ((bf16[8,1,64,512]{3,2,1,0:T(8,128)(2,1)}), bf16[8,1,64,512]{3,2,1,0:T(8,128)(2,1)}, u32[]{:S(2)}, u32[]{:S(2)}) async-start(bf16[8,1,64,512]{3,2,1,0:T(8,128)(2,1)} %copy.384), calls=%async_computation.12 | async-start | bytes 1048576 | tf_op jit(solution)/shard_map/all_to_all | solution.py:451
  526.3 12.3 %all-to-all-start.7 = ((bf16[8,1,64,128]{3,2,1,0:T(8,128)(2,1)}), bf16[8,1,64,128]{3,2,1,0:T(8,128)(2,1)}, u32[]{:S(2)}, u32[]{:S(2)}) async-start(bf16[8,1,64,128]{3,2,1,0:T(8,128)(2,1)} %copy.378), calls=%async_computation.10 | async-start | bytes 262144 | tf_op jit(solution)/shard_map/all_to_all | solution.py:437
  538.6 23.8 %all-to-all-start.5 = ((bf16[8,1,512,192]{2,3,1,0:T(8,128)(2,1)}), bf16[8,1,512,192]{2,3,1,0:T(8,128)(2,1)}, u32[]{:S(2)}, u32[]{:S(2)}) async-start(bf16[8,1,512,192]{2,3,1,0:T(8,128)(2,1)} %copy.372), calls=%async_computation.8 | async-start | bytes 3145728 | tf_op jit(solution)/shard_map/all_to_all | solution.py:423
  (36 other events, 179.1 us)
Sparse Core Ops, SparseCore 0:
  141.9 45.8 all-gather.2
  190.9 60.8 all-gather.4
  350.3 41.2 reduce-scatter.5
  396.2 128.6 all-reduce.3
  528.9 89.9 reduce-scatter.3
  623.0 88.6 reduce-scatter.7
where the time goes:
time: 731 us; the launch traced here: 721 us
  waiting for transfers between devices  269 us (37%)
  blocking collectives  141 us (19%)
  matrix products  134 us (18%)
  local copies, waits for them, and re-layouts  71.6 us (10%)
  starting transfers between devices  44.2 us (6%)
  other arithmetic  33.2 us (5%)
  between operations  15.6 us (2%)
  loops' own time  12.6 us (2%)
    reduce_scatter x1, waiting for transfers between devices, body(): lax.psum_scatter(input_part.astype(jnp.bfloat16), 'tp', scatter_dimension...  90.9 us
    psum x1, blocking collectives, body(): low_sum, out_sum = lax.psum((lowrank_portion, out_part), 'tp')  71 us
    psum x1, blocking collectives, body(): lax.psum(jnp.einsum('bkc,bcr->bkr', out_blocks, output_down_map, preferre...  69.5 us
    reduce_scatter x1, waiting for transfers between devices, body(): lax.psum_scatter(jnp.dot(attn_out, output_projection, preferred_element_t...  51.5 us
    reduce_scatter x1, waiting for transfers between devices, body(): lax.psum_scatter(kv_partial.astype(jnp.bfloat16), 'ctx', scatter_dimensio...  39.6 us
    dot_general x12, matrix products, masked_scores(): jnp.einsum('qd,kd->qk', query_rows, key_rows, preferred_element_type=jnp....  31.4 us
    unnamed x97, local copies, waits for them, and re-layouts  16.6 us
  transfers between devices with their start and end apart: 18, of which 15 were waited for; matrix products, arithmetic and copies ran while one was open for 18% of the time, Pallas kernels for 0%

commit v1 on v0

v1 whole, which is shorter than its diff:
```python
import functools
import math

import jax
import jax.numpy as jnp
from jax import lax
from jax.experimental import pallas as pl
from jax.experimental.pallas import tpu as pltpu
from jax.sharding import PartitionSpec as P

HEAD = 128
RANK = 64
BLK = 128
NEG = -1e30
ROPE_BASE = 1000000.0
F32 = jnp.float32
BF16 = jnp.bfloat16
MESH = pl.DeviceIdType.MESH
VMEM = pltpu.VMEM


def nn(a, b):
    return lax.dot_general(a, b, (((1,), (0,)), ((), ())), preferred_element_type=F32)


def nt(a, b):
    return lax.dot_general(a, b, (((1,), (1,)), ((), ())), preferred_element_type=F32)


class Dims:
    def __init__(self, rows, width, heads):
        self.rows = rows
        self.width = width
        self.heads = heads
        self.blocks = rows // BLK
        self.v = width
        self.qu = self.v + width // 2
        self.kvu = self.qu + heads * RANK
        self.od = self.kvu + RANK
        self.ou = self.od + HEAD
        self.total = self.ou + (width // HEAD) * RANK


def any_spec():
    return pl.BlockSpec(memory_space=pl.ANY)


def vmem_spec():
    return pl.BlockSpec(memory_space=VMEM)


def cost(flops, moved):
    return pl.CostEstimate(flops=int(flops), bytes_accessed=int(moved), transcendentals=0)


def serve_body(dim, index_ref, down, q_up, kv_up, o_down, o_up, out):
    half = dim.width // 2
    out[0, 0 : dim.width, :] = down[0, :, 0:HEAD]
    out[0, dim.v : dim.v + half, 0:RANK] = down[0, 0:half, HEAD:]
    out[0, dim.v : dim.v + half, RANK:] = down[0, half:, HEAD:]
    for head in range(dim.heads):
        at = dim.qu + head * RANK
        out[0, at : at + RANK, :] = q_up[0, :, head * HEAD : (head + 1) * HEAD]
        out[0, dim.od : dim.od + HEAD, head * RANK : (head + 1) * RANK] = o_down[
            0, head * HEAD : (head + 1) * HEAD, :
        ]
    out[0, dim.kvu : dim.kvu + RANK, :] = kv_up[0]
    for chunk in range(dim.width // HEAD):
        at = dim.ou + chunk * RANK
        out[0, at : at + RANK, :] = o_up[0, :, chunk * HEAD : (chunk + 1) * HEAD]


def serve(dim, index, down, q_up, kv_up, o_down, o_up):
    count = index.shape[0]

    def picked(array):
        return pl.BlockSpec((1,) + array.shape[1:], lambda i, idx: (idx[i], 0, 0))

    return pl.pallas_call(
        functools.partial(serve_body, dim),
        out_shape=jax.ShapeDtypeStruct((count, dim.total, HEAD), BF16),
        grid_spec=pltpu.PrefetchScalarGridSpec(
            num_scalar_prefetch=1,
            grid=(count,),
            in_specs=[picked(a) for a in (down, q_up, kv_up, o_down, o_up)],
            out_specs=pl.BlockSpec((1, dim.total, HEAD), lambda i, idx: (i, 0, 0)),
        ),
        cost_estimate=cost(0, 2 * count * dim.total * HEAD * 2),
        name="serve",
    )(index, down, q_up, kv_up, o_down, o_up)


def low_parts_body(dim, index_ref, fetched, x, cot, part, maps):
    half = dim.width // 2
    m = fetched.at[0]
    xb = x[...]
    part[0] = nn(xb, m[0 : dim.width, :]).astype(BF16)
    vv = m[dim.v : dim.v + half, :]
    low_v = nn(xb[:, :half], vv)[:, :RANK] + nn(xb[:, half:], vv)[:, RANK:]
    low_o = jnp.zeros((BLK, RANK), F32)
    for chunk in range(dim.width // HEAD):
        at = dim.ou + chunk * RANK
        low_o += nt(cot[:, chunk * HEAD : (chunk + 1) * HEAD], m[at : at + RANK, :])
    part[1] = jnp.concatenate([low_v, low_o], axis=1).astype(BF16)
    maps[...] = fetched[...]


def low_parts(dim, index, fetched, hidden, cot):
    return pl.pallas_call(
        functools.partial(low_parts_body, dim),
        out_shape=(
            jax.ShapeDtypeStruct((2, dim.rows, HEAD), BF16),
            jax.ShapeDtypeStruct((dim.blocks, dim.total, HEAD), BF16),
        ),
        grid_spec=pltpu.PrefetchScalarGridSpec(
            num_scalar_prefetch=1,
            grid=(dim.blocks,),
            in_specs=[
                pl.BlockSpec((1, dim.total, HEAD), lambda b, idx: (idx[b], 0, 0)),
                pl.BlockSpec((BLK, dim.width), lambda b, idx: (b, idx[dim.blocks])),
                pl.BlockSpec((BLK, dim.width), lambda b, idx: (b, 0)),
            ],
            out_specs=(
                pl.BlockSpec((2, BLK, HEAD), lambda b, idx: (0, b, 0)),
                pl.BlockSpec((1, dim.total, HEAD), lambda b, idx: (b, 0, 0)),
            ),
        ),
        cost_estimate=cost(2 * dim.rows * dim.width * 256, 3 * dim.total * HEAD * 4),
        name="low_parts",
    )(index, fetched, hidden, cot)


def sum_tp_body(n, x_ref, o_ref, recv, own, send_a, recv_a, send_b, recv_b):
    me = lax.axis_index("tp")
    row = lax.axis_index("ctx")
    barrier = pltpu.get_barrier_semaphore()
    for k in range(1, n):
        pl.semaphore_signal(
            barrier, inc=1, device_id=(row, lax.rem(me + k, n)), device_id_type=MESH
        )
    pl.semaphore_wait(barrier, n - 1)
    first = []
    for k in range(1, n):
        peer = lax.rem(me + k, n)
        copy = pltpu.make_async_remote_copy(
            src_ref=x_ref.at[peer],
            dst_ref=recv.at[k],
            send_sem=send_a.at[k],
            recv_sem=recv_a.at[k],
            device_id=(row, peer),
            device_id_type=MESH,
        )
        copy.start()
        first.append(copy)
    total = x_ref[me].astype(F32)
    for k in range(1, n):
        first[k - 1].wait_recv()
        total = total + recv[k].astype(F32)
    own[...] = total.astype(BF16)
    o_ref[me] = total.astype(BF16)
    second = []
    for k in range(1, n):
        peer = lax.rem(me + k, n)
        copy = pltpu.make_async_remote_copy(
            src_ref=own,
            dst_ref=o_ref.at[me],
            send_sem=send_b.at[k],
            recv_sem=recv_b.at[k],
            device_id=(row, peer),
            device_id_type=MESH,
        )
        copy.start()
        second.append(copy)
    for k in range(1, n):
        first[k - 1].wait_send()
        second[k - 1].wait()


def sum_tp(part, collective_id):
    n = lax.axis_size("tp")
    shape = part.shape
    piece = part.size // HEAD // n
    x = part.reshape(n, piece, HEAD)
    out = pl.pallas_call(
        functools.partial(sum_tp_body, n),
        out_shape=jax.ShapeDtypeStruct((n, piece, HEAD), BF16),
        in_specs=[vmem_spec()],
        out_specs=vmem_spec(),
        scratch_shapes=[
            pltpu.VMEM((n, piece, HEAD), BF16),
            pltpu.VMEM((piece, HEAD), BF16),
            pltpu.SemaphoreType.DMA((n,)),
            pltpu.SemaphoreType.DMA((n,)),
            pltpu.SemaphoreType.DMA((n,)),
            pltpu.SemaphoreType.DMA((n,)),
        ],
        compiler_params=pltpu.CompilerParams(collective_id=collective_id, has_side_effects=True),
        cost_estimate=cost(3e9, 3e7),
        name="sum_tp",
    )(x)
    return out.reshape(shape)


def finalize_body(dim, xq, xkv, low, maps, ctab, stab, q_out, kv_out, delta_out):
    core = lax.rem(lax.axis_index("tp"), 2)
    is_value = core == 1
    for b in range(dim.blocks):
        rows = slice(b * BLK, (b + 1) * BLK)
        m = maps.at[b]
        first = low[0, rows, :]
        second = low[1, rows, :]
        low_q = first[:, :RANK]
        low_kv = jnp.where(is_value, second[:, :RANK], first[:, RANK:])
        low_o = second[:, RANK:]
        cosine = ctab[rows, :]
        sine = stab[rows, :]
        for head in range(dim.heads):
            cols = slice(head * HEAD, (head + 1) * HEAD)
            at = dim.qu + head * RANK
            q = xq[rows, cols] + nn(low_q, m[at : at + RANK, :])
            q_out[rows, cols] = (q * cosine + pltpu.roll(q, HEAD // 2, 1) * sine).astype(BF16)
            lane = slice(head * RANK, (head + 1) * RANK)
            delta_out[rows, cols] = nt(low_o, m[dim.od : dim.od + HEAD, lane])
        kv = xkv[rows, :] + nn(low_kv, m[dim.kvu : dim.kvu + RANK, :])
        kv = kv.astype(BF16).astype(F32)
        turned = kv * cosine + pltpu.roll(kv, HEAD // 2, 1) * sine
        kv_out[rows, :] = jnp.where(is_value, kv, turned).astype(BF16)


def finalize(dim, xq, xkv, low, maps, ctab, stab):
    cols = dim.heads * HEAD
    return pl.pallas_call(
        functools.partial(finalize_body, dim),
        out_shape=(
            jax.ShapeDtypeStruct((dim.rows, cols), BF16),
            jax.ShapeDtypeStruct((dim.rows, HEAD), BF16),
            jax.ShapeDtypeStruct((dim.rows, cols), F32),
        ),
        in_specs=[vmem_spec()] * 6,
        out_specs=(vmem_spec(),) * 3,
        cost_estimate=cost(1e8, 4e6),
        name="finalize",
    )(xq, xkv, low, maps, ctab, stab)


def gather_kv_body(n, x_ref, o_ref, send_a, recv_a, send_b, recv_b):
    c = lax.axis_index("ctx")
    t = lax.axis_index("tp")
    core = lax.rem(t, 2)
    partner = t + 1 - 2 * core
    barrier = pltpu.get_barrier_semaphore()
    pl.semaphore_signal(barrier, inc=1, device_id=(c, partner), device_id_type=MESH)
    for k in range(1, n):
        pl.semaphore_signal(barrier, inc=1, device_id=(lax.rem(c + k, n), t), device_id_type=MESH)
    pl.semaphore_wait(barrier, n)
    copies = []
    for k in range(1, n):
        copy = pltpu.make_async_remote_copy(
            src_ref=x_ref,
            dst_ref=o_ref.at[core, c],
            send_sem=send_a.at[k],
            recv_sem=recv_a.at[k],
            device_id=(lax.rem(c + k, n), t),
            device_id_type=MESH,
        )
        copy.start()
        copies.append(copy)
    forwards = []
    copy = pltpu.make_async_remote_copy(
        src_ref=x_ref,
        dst_ref=o_ref.at[core, c],
        send_sem=send_b.at[0],
        recv_sem=recv_b.at[0],
        device_id=(c, partner),
        device_id_type=MESH,
    )
    copy.start()
    forwards.append(copy)
    o_ref[core, c] = x_ref[...]
    for k in range(1, n):
        source = lax.rem(c - k + n, n)
        copies[k - 1].wait_recv()
        copy = pltpu.make_async_remote_copy(
            src_ref=o_ref.at[core, source],
            dst_ref=o_ref.at[core, source],
            send_sem=send_b.at[k],
            recv_sem=recv_b.at[k],
            device_id=(c, partner),
            device_id_type=MESH,
        )
        copy.start()
        forwards.append(copy)
    for k in range(1, n):
        copies[k - 1].wait_send()
    for copy in forwards:
        copy.wait()


def gather_kv(kv, collective_id):
    n = lax.axis_size("ctx")
    rows = kv.shape[0]
    return pl.pallas_call(
        functools.partial(gather_kv_body, n),
        out_shape=jax.ShapeDtypeStruct((2, n, rows, HEAD), BF16),
        in_specs=[vmem_spec()],
        out_specs=vmem_spec(),
        scratch_shapes=[pltpu.SemaphoreType.DMA((n,))] * 4,
        compiler_params=pltpu.CompilerParams(collective_id=collective_id, has_side_effects=True),
        cost_estimate=cost(3e9, 3e7),
        name="gather_kv",
    )(kv)


def allowed_tile(j, rows, first_pos, start):
    key_pos = j * rows + lax.broadcasted_iota(jnp.int32, (rows, rows), 0)
    query_pos = first_pos + lax.broadcasted_iota(jnp.int32, (1, rows), 1)
    return (key_pos <= query_pos) & (key_pos >= start)


def attend_body(dim, meta, start_ref, q_ref, kv_ref, o_ref, lse_ref, s_scr, acc):
    rows = dim.rows
    scale = HEAD ** (-0.5)
    lo = meta[0]
    hi = meta[1]
    first_pos = meta[2]
    start = start_ref[...]
    heads = range(dim.heads)

    def scores(j, peaks):
        kj = kv_ref[0, j]
        ok = allowed_tile(j, rows, first_pos, start)
        fresh = []
        for h in heads:
            s = nt(kj, q_ref[:, h * HEAD : (h + 1) * HEAD]) * scale
            s = jnp.where(ok, s, NEG)
            s_scr[h, j] = s
            fresh.append(jnp.maximum(peaks[h], jnp.max(s, axis=0, keepdims=True)))
        return tuple(fresh)

    peaks = lax.fori_loop(lo, hi, scores, tuple(jnp.full((1, rows), NEG, F32) for h in heads))
    acc[...] = jnp.zeros_like(acc)

    def mix(j, sums):
        vt = kv_ref[1, j].T
        fresh = []
        for h in heads:
            p = jnp.exp(s_scr[h, j] - peaks[h])
            fresh.append(sums[h] + jnp.sum(p, axis=0, keepdims=True))
            acc[h] += nn(vt, p.astype(BF16))
        return tuple(fresh)

    sums = lax.fori_loop(lo, hi, mix, tuple(jnp.zeros((1, rows), F32) for h in heads))
    for h in heads:
        o_ref[:, h * HEAD : (h + 1) * HEAD] = (acc[h] / sums[h]).T.astype(BF16)
        lse_ref[h] = peaks[h] + jnp.log(sums[h])


def attend(dim, meta, start, q, kv):
    n = kv.shape[1]
    rows = dim.rows
    return pl.pallas_call(
        functools.partial(attend_body, dim),
        out_shape=(
            jax.ShapeDtypeStruct(q.shape, BF16),
            jax.ShapeDtypeStruct((dim.heads, 1, rows), F32),
        ),
        in_specs=[pl.BlockSpec(memory_space=pltpu.SMEM)] + [vmem_spec()] * 3,
        out_specs=(vmem_spec(), vmem_spec()),
        scratch_shapes=[
            pltpu.VMEM((dim.heads, n, rows, rows), F32),
            pltpu.VMEM((dim.heads, HEAD, rows), F32),
        ],
        compiler_params=pltpu.CompilerParams(vmem_limit_bytes=40 << 20),
        cost_estimate=cost(4 * dim.heads * rows * rows * n * HEAD * 4, 3e7),
        name="attend",
    )(meta, start, q, kv)


def attend_back_body(
    dim, n, meta, start_ref, q_ref, kv_ref, o_ref, lse_ref, do_ref, ctab, stab, dq_ref, dkv_ref, acc
):
    rows = dim.rows
    scale = HEAD ** (-0.5)
    lo = meta[0]
    hi = meta[1]
    first_pos = meta[2]
    start = start_ref[...]
    heads = range(dim.heads)
    acc[...] = jnp.zeros_like(acc)

    def clear(j, carry):
        dkv_ref[0, j] = jnp.zeros((rows, HEAD), BF16)
        dkv_ref[1, j] = jnp.zeros((rows, HEAD), BF16)
        return carry

    lax.fori_loop(0, lo, clear, 0)
    lax.fori_loop(hi, n, clear, 0)
    delta = []
    for h in heads:
        cols = slice(h * HEAD, (h + 1) * HEAD)
        both = do_ref[:, cols].astype(F32) * o_ref[:, cols].astype(F32)
        delta.append(jnp.sum(both.T, axis=0, keepdims=True))

    def step(j, carry):
        kj = kv_ref[0, j]
        vj = kv_ref[1, j]
        kt = kj.T
        ok = allowed_tile(j, rows, first_pos, start)
        dk = jnp.zeros((rows, HEAD), F32)
        dv = jnp.zeros((rows, HEAD), F32)
        for h in heads:
            qh = q_ref[:, h * HEAD : (h + 1) * HEAD]
            doh = do_ref[:, h * HEAD : (h + 1) * HEAD]
            s = jnp.where(ok, nt(kj, qh) * scale, NEG)
            p = jnp.exp(s - lse_ref[h])
            ds = (p * (nt(vj, doh) - delta[h])).astype(BF16)
            acc[h] += nn(kt, ds)
            dk += nn(ds, qh)
            dv += nn(p.astype(BF16), doh)
        dkv_ref[0, j] = (dk * scale).astype(BF16)
        dkv_ref[1, j] = dv.astype(BF16)
        return carry

    lax.fori_loop(lo, hi, step, 0)
    for h in heads:
        dq = (acc[h] * scale).T
        dq = dq * ctab[...] - pltpu.roll(dq, HEAD // 2, 1) * stab[...]
        dq_ref[:, h * HEAD : (h + 1) * HEAD] = dq.astype(BF16)


def attend_back(dim, meta, start, q, kv, out, lse, grad, ctab, stab):
    n = kv.shape[1]
    rows = dim.rows
    return pl.pallas_call(
        functools.partial(attend_back_body, dim, n),
        out_shape=(
            jax.ShapeDtypeStruct(q.shape, BF16),
            jax.ShapeDtypeStruct(kv.shape, BF16),
        ),
        in_specs=[pl.BlockSpec(memory_space=pltpu.SMEM)] + [vmem_spec()] * 8,
        out_specs=(vmem_spec(), vmem_spec()),
        scratch_shapes=[pltpu.VMEM((dim.heads, HEAD, rows), F32)],
        compiler_params=pltpu.CompilerParams(vmem_limit_bytes=40 << 20),
        cost_estimate=cost(10 * dim.heads * rows * rows * n * HEAD * 4, 3e7),
        name="attend_back",
    )(meta, start, q, kv, out, lse, grad, ctab, stab)


def scatter_kv_body(
    n, x_ref, ctab, stab, o_ref, half, mine, arrived, send_a, recv_a, send_b, recv_b
):
    c = lax.axis_index("ctx")
    t = lax.axis_index("tp")
    core = lax.rem(t, 2)
    partner = t + 1 - 2 * core
    barrier = pltpu.get_barrier_semaphore()
    pl.semaphore_signal(barrier, inc=1, device_id=(c, partner), device_id_type=MESH)
    for k in range(1, n):
        pl.semaphore_signal(barrier, inc=1, device_id=(lax.rem(c + k, n), t), device_id_type=MESH)
    pl.semaphore_wait(barrier, n)
    order = list(range(1, n)) + [0]
    swaps = {}
    for k in order:
        copy = pltpu.make_async_remote_copy(
            src_ref=x_ref.at[1 - core, lax.rem(c + k, n)],
            dst_ref=half.at[k],
            send_sem=send_a.at[k],
            recv_sem=recv_a.at[k],
            device_id=(c, partner),
            device_id_type=MESH,
        )
        copy.start()
        swaps[k] = copy
    sends = {}
    for k in range(1, n):
        swaps[k].wait_recv()
        mine[k] = (
            x_ref[core, lax.rem(c + k, n)].astype(F32) + half[k].astype(F32)
        ).astype(BF16)
        copy = pltpu.make_async_remote_copy(
            src_ref=mine.at[k],
            dst_ref=arrived.at[k],
            send_sem=send_b.at[k],
            recv_sem=recv_b.at[k],
            device_id=(lax.rem(c + k, n), t),
            device_id_type=MESH,
        )
        copy.start()
        sends[k] = copy
    swaps[0].wait_recv()
    total = x_ref[core, c].astype(F32) + half[0].astype(F32)
    for k in range(1, n):
        sends[k].wait_recv()
        total = total + arrived[k].astype(F32)
    turned = total * ctab[...] - pltpu.roll(total, HEAD // 2, 1) * stab[...]
    o_ref[...] = jnp.where(core == 1, total, turned).astype(BF16)
    for k in order:
        swaps[k].wait_send()
    for k in range(1, n):
        sends[k].wait_send()


def scatter_kv(grads, ctab, stab, collective_id):
    n = grads.shape[1]
    rows = grads.shape[2]
    return pl.pallas_call(
        functools.partial(scatter_kv_body, n),
        out_shape=jax.ShapeDtypeStruct((rows, HEAD), BF16),
        in_specs=[vmem_spec()] * 3,
        out_specs=vmem_spec(),
        scratch_shapes=[
            pltpu.VMEM((n, rows, HEAD), BF16),
            pltpu.VMEM((n, rows, HEAD), BF16),
            pltpu.VMEM((n, rows, HEAD), BF16),
        ]
        + [pltpu.SemaphoreType.DMA((n,))] * 4,
        compiler_params=pltpu.CompilerParams(collective_id=collective_id, has_side_effects=True),
        cost_estimate=cost(3e9, 3e7),
        name="scatter_kv",
    )(grads, ctab, stab)


def low_grads_body(dim, attn, grad_q, grad_kv, maps, part):
    core = lax.rem(lax.axis_index("tp"), 2)
    m = maps.at[0]
    low_q = jnp.zeros((BLK, RANK), F32)
    low_out = jnp.zeros((BLK, RANK), F32)
    for head in range(dim.heads):
        cols = slice(head * HEAD, (head + 1) * HEAD)
        lane = slice(head * RANK, (head + 1) * RANK)
        at = dim.qu + head * RANK
        low_q += nt(grad_q[:, cols], m[at : at + RANK, :])
        low_out += nn(attn[:, cols], m[dim.od : dim.od + HEAD, lane])
    low_kv = nt(grad_kv[...], m[dim.kvu : dim.kvu + RANK, :])
    zero = jnp.zeros_like(low_kv)
    low_k = jnp.where(core == 0, low_kv, zero)
    low_v = jnp.where(core == 1, low_kv, zero)
    part[0] = jnp.concatenate([low_q, low_k], axis=1).astype(BF16)
    part[1] = jnp.concatenate([low_v, low_out], axis=1).astype(BF16)


def low_grads(dim, attn, grad_q, grad_kv, maps):
    cols = dim.heads * HEAD
    return pl.pallas_call(
        functools.partial(low_grads_body, dim),
        out_shape=jax.ShapeDtypeStruct((2, dim.rows, HEAD), BF16),
        grid=(dim.blocks,),
        in_specs=[
            pl.BlockSpec((BLK, cols), lambda b: (b, 0)),
            pl.BlockSpec((BLK, cols), lambda b: (b, 0)),
            pl.BlockSpec((BLK, HEAD), lambda b: (b, 0)),
            pl.BlockSpec((1, dim.total, HEAD), lambda b: (b, 0, 0)),
        ],
        out_specs=pl.BlockSpec((2, BLK, HEAD), lambda b: (0, b, 0)),
        cost_estimate=cost(1e8, 4e6),
        name="low_grads",
    )(attn, grad_q, grad_kv, maps)


def block_grads_body(
    dim, index_ref, x, cot, low_in, low_grad, attn, grad_q, grad_kv, maps, out, d_in, d_out
):
    half = dim.width // 2
    core = lax.rem(lax.axis_index("tp"), 2)
    m = maps.at[0]
    low_qk_t = low_in[0].T
    low_vo_t = low_in[1].T
    low_q_t = low_qk_t[:RANK]
    low_kv_t = jnp.where(core == 1, low_vo_t[:RANK], low_qk_t[RANK:])
    low_o = low_in[1, :, RANK:]
    g_qk = low_grad[0]
    g_v = low_grad[1, :, :RANK]
    low_out = low_grad[1, :, RANK:]
    low_out_t = low_out.T
    xt = x[...].T
    out[0, 0 : dim.width, :] = nn(xt, g_qk).astype(BF16)
    up = nn(xt, g_v).astype(BF16)
    out[0, dim.v : dim.v + half, 0:RANK] = up[:half]
    out[0, dim.v : dim.v + half, RANK:] = up[half:]
    for head in range(dim.heads):
        cols = slice(head * HEAD, (head + 1) * HEAD)
        lane = slice(head * RANK, (head + 1) * RANK)
        at = dim.qu + head * RANK
        out[0, at : at + RANK, :] = nn(low_q_t, grad_q[:, cols]).astype(BF16)
        out[0, dim.od : dim.od + HEAD, lane] = nn(attn[:, cols].T, low_o).astype(BF16)
    out[0, dim.kvu : dim.kvu + RANK, :] = nn(low_kv_t, grad_kv[...]).astype(BF16)
    for chunk in range(dim.width // HEAD):
        cols = slice(chunk * HEAD, (chunk + 1) * HEAD)
        at = dim.ou + chunk * RANK
        out[0, at : at + RANK, :] = nn(low_out_t, cot[:, cols]).astype(BF16)
        d_out[:, cols] = nn(low_out, m[at : at + RANK, :])
    vv = m[dim.v : dim.v + half, :]
    d_qk = nt(g_qk, m[0 : dim.width, :])
    d_in[:, :half] = d_qk[:, :half] + nt(g_v, vv[:, :RANK])
    d_in[:, half:] = d_qk[:, half:] + nt(g_v, vv[:, RANK:])


def block_grads(dim, index, owners, hidden, cot, low_in, low_grad, attn, grad_q, grad_kv, maps):
    cols = dim.heads * HEAD
    low_spec = pl.BlockSpec((2, BLK, HEAD), lambda b, idx: (0, b, 0))
    wide_spec = pl.BlockSpec((BLK, dim.width), lambda b, idx: (b, 0))
    return pl.pallas_call(
        functools.partial(block_grads_body, dim),
        out_shape=(
            jax.ShapeDtypeStruct((owners, dim.total, HEAD), BF16),
            jax.ShapeDtypeStruct((dim.rows, dim.width), F32),
            jax.ShapeDtypeStruct((dim.rows, dim.width), F32),
        ),
        grid_spec=pltpu.PrefetchScalarGridSpec(
            num_scalar_prefetch=1,
            grid=(dim.blocks,),
            in_specs=[
                pl.BlockSpec((BLK, dim.width), lambda b, idx: (b, idx[dim.blocks])),
                wide_spec,
                low_spec,
                low_spec,
                pl.BlockSpec((BLK, cols), lambda b, idx: (b, 0)),
                pl.BlockSpec((BLK, cols), lambda b, idx: (b, 0)),
                pl.BlockSpec((BLK, HEAD), lambda b, idx: (b, 0)),
                pl.BlockSpec((1, dim.total, HEAD), lambda b, idx: (b, 0, 0)),
            ],
            out_specs=(
                pl.BlockSpec((1, dim.total, HEAD), lambda b, idx: (idx[b], 0, 0)),
                wide_spec,
                wide_spec,
            ),
        ),
        cost_estimate=cost(1e9, 6e6),
        name="block_grads",
    )(index, hidden, cot, low_in, low_grad, attn, grad_q, grad_kv, maps)


def store_body(dim, count, row_ref, arrived, down, q_up, kv_up, o_down, o_up, acc):
    half = dim.width // 2
    i = pl.program_id(0)

    @pl.when(i == 0)
    def _():
        acc[...] = jnp.zeros_like(acc)

    row = row_ref[i]

    @pl.when(row >= 0)
    def _():
        acc[row] += arrived[0].astype(F32)

    @pl.when(i == count - 1)
    def _():
        for s in range(acc.shape[0]):
            down[s, :, 0:HEAD] = acc[s, 0 : dim.width, :]
            down[s, :half, HEAD:] = acc[s, dim.v : dim.v + half, :RANK]
            down[s, half:, HEAD:] = acc[s, dim.v : dim.v + half, RANK:]
            for head in range(dim.heads):
                cols = slice(head * HEAD, (head + 1) * HEAD)
                at = dim.qu + head * RANK
                q_up[s, :, cols] = acc[s, at : at + RANK, :]
                o_down[s, cols, :] = acc[
                    s, dim.od : dim.od + HEAD, head * RANK : (head + 1) * RANK
                ]
            kv_up[s] = acc[s, dim.kvu : dim.kvu + RANK, :]
            for chunk in range(dim.width // HEAD):
                at = dim.ou + chunk * RANK
                o_up[s, :, chunk * HEAD : (chunk + 1) * HEAD] = acc[s, at : at + RANK, :]


def to_store(dim, rows, arrived, shapes):
    count = arrived.shape[0]
    tenants = shapes[0][0]

    def whole(shape):
        return pl.BlockSpec(shape, lambda i, idx: (0, 0, 0))

    return pl.pallas_call(
        functools.partial(store_body, dim, count),
        out_shape=tuple(jax.ShapeDtypeStruct(s, F32) for s in shapes),
        grid_spec=pltpu.PrefetchScalarGridSpec(
            num_scalar_prefetch=1,
            grid=(count,),
            in_specs=[pl.BlockSpec((1, dim.total, HEAD), lambda i, idx: (i, 0, 0))],
            out_specs=tuple(whole(s) for s in shapes),
            scratch_shapes=[pltpu.VMEM((tenants, dim.total, HEAD), F32)],
        ),
        cost_estimate=cost(0, 6e6),
        name="to_store",
    )(rows, arrived)


def body(
    hidden_input,
    output_cotangent,
    query_projection,
    key_value_projection,
    output_projection,
    adapter_qkv_down_store,
    adapter_query_up,
    adapter_key_value_up,
    adapter_output_down,
    adapter_output_up,
    crop_token_length,
    tenant_per_block,
    tenant_store_row,
):
    ctx_count = lax.axis_size("ctx")
    ctx_index = lax.axis_index("ctx")
    tp_index = lax.axis_index("tp")
    rows_dev = hidden_input.shape[0]
    out_cols = output_cotangent.shape[1]
    tenants = adapter_qkv_down_store.shape[0]
    dim = Dims(rows_dev, out_cols, query_projection.shape[1] // HEAD)
    stores = (
        adapter_qkv_down_store,
        adapter_query_up,
        adapter_key_value_up,
        adapter_output_down,
        adapter_output_up,
    )

    tenant_ids = jnp.arange(tenant_store_row.shape[0], dtype=jnp.int32)
    rows_per_block = jnp.sum(
        jnp.where(tenant_per_block[:, None] == tenant_ids[None, :], tenant_store_row[None, :], 0),
        axis=1,
    )
    shard_rows = rows_per_block.reshape(ctx_count, dim.blocks)
    shard_owner = shard_rows // tenants
    served = shard_owner == ctx_index
    served_row = jnp.max(jnp.where(served, shard_rows - ctx_index * tenants, -1), axis=1)
    serve_index = jnp.maximum(served_row, 0)
    my_owner = lax.dynamic_index_in_dim(shard_owner, ctx_index, 0, keepdims=False)
    pick_index = jnp.concatenate([my_owner, tp_index[None]]).astype(jnp.int32)

    my_pos = ctx_index * rows_dev + jnp.arange(rows_dev, dtype=jnp.int32)
    crop_ends = jnp.cumsum(crop_token_length)
    row_start = jnp.max(
        jnp.where(crop_ends[:, None] <= my_pos[None, :], crop_ends[:, None], 0), axis=0
    ).astype(jnp.int32)
    first_pos = ctx_index * rows_dev
    first_start = jnp.max(jnp.where(crop_ends <= first_pos, crop_ends, 0))
    meta = jnp.stack([first_start // rows_dev, ctx_index + 1, first_pos]).astype(jnp.int32)
    start = row_start[None, :]
    half_dim = HEAD // 2
    exponent = jnp.arange(half_dim, dtype=F32) * (2.0 / HEAD)
    frequency = jnp.exp(-exponent * math.log(ROPE_BASE))
    angles = my_pos.astype(F32)[:, None] * jnp.concatenate([frequency, frequency])[None, :]
    sign = jnp.where(jnp.arange(HEAD) < half_dim, -1.0, 1.0).astype(F32)
    ctab = jnp.cos(angles)
    stab = jnp.sin(angles) * sign[None, :]

    fetched = lax.all_to_all(
        serve(dim, serve_index, *stores), "ctx", split_axis=0, concat_axis=0, tiled=True
    )
    pieces = lax.all_gather(output_cotangent, "tp", axis=1, tiled=True)
    xq = jnp.dot(hidden_input, query_projection, preferred_element_type=F32)
    xkv = jnp.dot(hidden_input, key_value_projection, preferred_element_type=F32)

    part, maps = low_parts(dim, pick_index, fetched, hidden_input, output_cotangent)
    low_in = sum_tp(part, 0)
    query, keyval, o_delta = finalize(dim, xq, xkv, low_in, maps, ctab, stab)
    kv_all = gather_kv(keyval, 1)
    attn, lse = attend(dim, meta, start, query, kv_all)

    heads_total = lax.psum_scatter(
        jnp.dot(attn, output_projection, preferred_element_type=F32).astype(BF16),
        "tp",
        scatter_dimension=1,
        tiled=True,
    ).astype(F32)

    grad_attn = (
        lax.dot_general(
            pieces, output_projection, (((1,), (1,)), ((), ())), preferred_element_type=F32
        )
        + o_delta
    ).astype(BF16)
    grad_q, grad_kv_all = attend_back(
        dim, meta, start, query, kv_all, attn, lse, grad_attn, ctab, stab
    )
    grad_kv = scatter_kv(grad_kv_all, ctab, stab, 2)

    low_grad = sum_tp(low_grads(dim, attn, grad_q, grad_kv, maps), 0)
    input_part = nt(grad_q, query_projection) + nt(grad_kv, key_value_projection)
    input_total = lax.psum_scatter(
        input_part.astype(BF16), "tp", scatter_dimension=1, tiled=True
    ).astype(F32)
    sent, d_in, d_out = block_grads(
        dim,
        pick_index,
        ctx_count,
        hidden_input,
        output_cotangent,
        low_in,
        low_grad,
        attn,
        grad_q,
        grad_kv,
        maps,
    )
    output = (heads_total + d_out).astype(BF16)
    hidden_input_gradient = (input_total + d_in).astype(BF16)
    returned = lax.all_to_all(sent, "ctx", split_axis=0, concat_axis=0, tiled=True)
    grads = to_store(dim, served_row, returned, [s.shape for s in stores])
    return (output, hidden_input_gradient) + tuple(grads)


def solution(mesh):
    in_specs = (
        P("ctx", None),
        P("ctx", "tp"),
        P(None, "tp"),
        P(None, "tp"),
        P("tp", None),
        P("ctx", "tp", None),
        P("ctx", None, "tp"),
        P("ctx", None, "tp"),
        P("ctx", "tp", None),
        P("ctx", None, "tp"),
        P(),
        P(),
        P(),
    )
    out_specs = (
        P("ctx", "tp"),
        P("ctx", "tp"),
        P("ctx", "tp", None),
        P("ctx", None, "tp"),
        P("ctx", None, "tp"),
        P("ctx", "tp", None),
        P("ctx", None, "tp"),
    )
    return jax.shard_map(body, mesh=mesh, in_specs=in_specs, out_specs=out_specs, check_vma=False)
```

time: 731 us -> 321 us (0.44); the launches traced: 721 us -> 320 us
  waiting for transfers between devices: 269 us -> 126 us
  blocking collectives: 141 us -> 0 us
  Pallas kernels: 0 us -> 117 us
  matrix products: 134 us -> 29.7 us
  local copies, waits for them, and re-layouts: 71.6 us -> 13 us
  starting transfers between devices: 44.2 us -> 9.79 us
  other arithmetic: 33.2 us -> 8.71 us
  loops' own time: 12.6 us -> 0 us
    psum x2 -> x0, blocking collectives: 141 us -> none  [the longest x1 71 us: body(): low_sum, out_sum = lax.psum((lowrank_portion, out_part), 'tp')]
    pallas_call x0 -> x12, Pallas kernels: none -> 117 us  [the longest x2 35.3 us: sum_tp(): pl.pallas_call(functools.partial(sum_tp_body, n), out_shape=jax.ShapeDtyp...]
    dot_general x86 -> x6, matrix products: 134 us -> 29.7 us  [the longest x2 8.57 us: nt(): lax.dot_general(a, b, (((1,), (1,)), ((), ())), preferred_element_type=F32)]
    reduce_scatter x3 -> x2, waiting for transfers between devices: 182 us -> 80.1 us  [the longest x1 61.9 us: body(): lax.psum_scatter(input_part.astype(BF16), 'tp', scatter_dimension=1, tile...]
    all_to_all x10 -> x2, starting transfers between devices: 43.4 us -> 9.68 us  [the longest x1 5.18 us: body(): lax.all_to_all(serve(dim, serve_index, *stores), 'ctx', split_axis=0, con...]
    dynamic_slice x38 -> x0, local copies, waits for them, and re-layouts: 25.9 us -> none  [the longest x18 13.6 us: key_block(): seg_block = lax.dynamic_slice_in_dim(key_seg, start_at, KBLK, 0)]
    all_to_all x10 -> x2, waiting for transfers between devices: 64.4 us -> 44.9 us  [the longest x1 29.5 us: body(): lax.all_to_all(serve(dim, serve_index, *stores), 'ctx', split_axis=0, con...]
    psum x1 -> x0, waiting for transfers between devices: 14.6 us -> none  [body(): lowrank_gradient = lax.psum(low_grad_part.astype(jnp.bfloat16), 'tp')]
  transfers between devices with their start and end apart: 18 -> 5, of which waited for: 15 -> 4; matrix products, arithmetic and copies ran while one was open for 18% -> 14% of each run, Pallas kernels for 0% -> 37%
where the time goes in v1:
time: 321 us; the launch traced here: 320 us
  waiting for transfers between devices  126 us (39%)
  Pallas kernels  117 us (36%)
  matrix products  29.7 us (9%)
  between operations  15.9 us (5%)
  local copies, waits for them, and re-layouts  13 us (4%)
  starting transfers between devices  9.79 us (3%)
  other arithmetic  8.71 us (3%)
    reduce_scatter x1, waiting for transfers between devices, body(): lax.psum_scatter(input_part.astype(BF16), 'tp', scatter_dimension=1, tile...  61.9 us
    pallas_call x2, Pallas kernels, sum_tp(): pl.pallas_call(functools.partial(sum_tp_body, n), out_shape=jax.ShapeDtyp...  35.3 us
    pallas_call x1, Pallas kernels, scatter_kv(): pl.pallas_call(functools.partial(scatter_kv_body, n), out_shape=jax.Shape...  30.2 us
    all_to_all x1, waiting for transfers between devices, body(): lax.all_to_all(serve(dim, serve_index, *stores), 'ctx', split_axis=0, con...  29.5 us
    reduce_scatter x1, waiting for transfers between devices, body(): lax.psum_scatter(jnp.dot(attn, output_projection, preferred_element_type=...  18.1 us
    pallas_call x1, Pallas kernels, gather_kv(): pl.pallas_call(functools.partial(gather_kv_body, n), out_shape=jax.ShapeD...  17 us
    all_to_all x1, waiting for transfers between devices, body(): lax.all_to_all(sent, 'ctx', split_axis=0, concat_axis=0, tiled=True)  15.4 us
    unnamed x36, local copies, waits for them, and re-layouts  12.9 us
  transfers between devices with their start and end apart: 5, of which 4 were waited for; matrix products, arithmetic and copies ran while one was open for 14% of the time, Pallas kernels for 37%

profile of v1, /device:TPU:0, one launch (start us, length us, event | category | flops | bytes accessed | tf_op | source)
XLA Modules:
  0.0 320.1 jit_solution(6378166706423927695)
XLA Ops:
  8.9 2.2 copy.28.down
  11.1 1.7 copy.29.o_down
  13.5 6.9 %serve.1 = bf16[8,1344,128]{2,1,0:T(8,128)(2,1)} custom-call(s32[8]{0:T(128)} %broadcast_maximum_fusion.index_ref, bf16[4,512,192]{2,1,0:T(8,128)(2,1)} %copy.28.down, bf16[4,64,256]{2,1,0:T(8,128)(2,1)} %q_up.1, bf16[4,64,128]{2,1,0:T(8,128)(2,1)} %kv_up.1, bf16[4,256,64]{2,1,0:T(8,128)(2,1)} %copy.29.o_down, bf16[4,64,512]{2,1,0:T(8,128)(2,1)} %o_up.1), custom_call_target="tpu_custom_call" | custom-call | bytes 5505024 | tf_op jit(solution)/shard_map/serve/pallas_call | solution.py:79
  20.4 5.2 %all-to-all-start = ((bf16[8,1344,128]{2,1,0:T(8,128)(2,1)}), bf16[8,1344,128]{2,1,0:T(8,128)(2,1)}, u32[]{:S(2)}, u32[]{:S(2)}) async-start(bf16[8,1344,128]{2,1,0:T(8,128)(2,1)} %serve.1), calls=%async_computation | async-start | bytes 5505024 | tf_op jit(solution)/shard_map/all_to_all | solution.py:748
  29.3 1.5 fusion.1
  30.8 5.4 %fusion.7.xkv = f32[384,128]{1,0:T(8,128)} fusion(bf16[384,8192]{1,0:T(8,128)(2,1)} %x.3, bf16[8192,128]{1,0:T(8,128)(2,1)S(1)} %copy-done), kind=kOutput, calls=%fused_computation.32 | convolution fusion | flops 805306368 | bytes 8585216 | tf_op jit(solution)/shard_map/dot_general | solution.py:753
  36.2 5.3 %fusion.6.xq = f32[384,256]{1,0:T(8,128)} fusion(bf16[384,8192]{1,0:T(8,128)(2,1)} %x.3, bf16[8192,256]{1,0:T(8,128)(2,1)S(1)} %copy-done.10), kind=kOutput, calls=%fused_computation.31 | convolution fusion | flops 1610612736 | bytes 10878976 | tf_op jit(solution)/shard_map/dot_general | solution.py:752
  41.5 29.5 %all-to-all-done.fetched = bf16[8,1344,128]{2,1,0:T(8,128)(2,1)} async-done(((bf16[8,1344,128]{2,1,0:T(8,128)(2,1)}), bf16[8,1344,128]{2,1,0:T(8,128)(2,1)}, u32[]{:S(2)}, u32[]{:S(2)}) %all-to-all-start) | async-done | bytes 2752544 | tf_op jit(solution)/shard_map/all_to_all | solution.py:748
  71.0 4.4 %low_parts.1 = (bf16[2,384,128]{2,1,0:T(8,128)(2,1)}, bf16[3,1344,128]{2,1,0:T(8,128)(2,1)}) custom-call(s32[4]{0:T(128)} %pad_add_fusion.1.index_ref, bf16[8,1344,128]{2,1,0:T(8,128)(2,1)} %all-to-all-done.fetched, bf16[384,8192]{1,0:T(8,128)(2,1)} %x.3, bf16[384,512]{1,0:T(8,128)(2,1)} %cot.3), custom_call_target="tpu_custom_call" | custom-call | flops 100663296 | bytes 2064384 | tf_op jit(solution)/shard_map/low_parts/pallas_call | solution.py:109
  75.4 18.3 %sum_tp.2 = bf16[16,48,128]{2,1,0:T(8,128)(2,1)} custom-call(bf16[16,48,128]{2,1,0:T(8,128)(2,1)} %bitcast.30), custom_call_target="tpu_custom_call" | custom-call | flops 3000000000 | bytes 30000000 | tf_op jit(solution)/shard_map/sum_tp/pallas_call | solution.py:184
  93.8 2.9 finalize.1
  96.7 17.0 %gather_kv.1.kv_ref = bf16[2,8,384,128]{3,2,1,0:T(8,128)(2,1)} custom-call(bf16[384,128]{1,0:T(8,128)(2,1)} %get-tuple-element.27.x_ref), custom_call_target="tpu_custom_call" | custom-call | flops 3000000000 | bytes 30000000 | tf_op jit(solution)/shard_map/gather_kv/pallas_call | solution.py:302
  113.7 1.4 copy-done.7
  115.1 1.5 attend.1
  117.3 4.5 %convolution_convert_fusion = bf16[384,8192]{1,0:T(8,128)(2,1)} fusion(bf16[384,256]{1,0:T(8,128)(2,1)S(1)} %get-tuple-element.28.o_ref.attn, bf16[256,8192]{1,0:T(8,128)(2,1)S(1)} %copy-done.9), kind=kOutput, calls=%fused_computation.1 | convolution fusion | flops 1613758464 | bytes 10682368 | tf_op jit(solution)/shard_map/dot_general | solution.py:762
  122.7 6.0 %fusion.do_ref = bf16[384,256]{1,0:T(8,128)(2,1)S(1)} fusion(f32[384,256]{1,0:T(8,128)S(1)} %copy-done.14, bf16[384,8192]{1,0:T(8,128)(2,1)} %all-gather.2.cloned.1.call-done, bf16[256,8192]{1,0:T(8,128)(2,1)} %param.17), kind=kOutput, calls=%fused_computation.3 | convolution fusion | flops 1610809344 | bytes 11075584 | tf_op jit(solution)/shard_map/dot_general | solution.py:769
  128.7 2.6 attend_back.1
  132.5 30.2 %scatter_kv.1.grad_kv = bf16[384,128]{1,0:T(8,128)(2,1)} custom-call(bf16[2,8,384,128]{3,2,1,0:T(8,128)(2,1)} %copy-done.6, f32[384,128]{1,0:T(8,128)} %get-tuple-element.65.ctab, f32[384,128]{1,0:T(8,128)} %get-tuple-element.64.stab), custom_call_target="tpu_custom_call" | custom-call | flops 3000000000 | bytes 30000000 | tf_op jit(solution)/shard_map/scatter_kv/pallas_call | solution.py:506
  162.8 4.1 %fusion.8 = f32[384,8192]{1,0:T(8,128)S(1)} fusion(bf16[384,256]{1,0:T(8,128)(2,1)S(1)} %get-tuple-element.31.grad_q, bf16[8192,256]{1,0:T(8,128)(2,1)} %param.15), kind=kOutput, calls=%fused_computation.33 | convolution fusion | flops 1610612736 | bytes 16973824 | tf_op jit(solution)/shard_map/dot_general | solution.py:27
  166.9 4.5 %add_convert_fusion = bf16[384,8192]{1,0:T(8,128)(2,1)} fusion(f32[384,8192]{1,0:T(8,128)S(1)} %fusion.8, bf16[384,128]{1,0:T(8,128)(2,1)S(1)} %copy-done.11, bf16[8192,128]{1,0:T(8,128)(2,1)S(1)} %copy-done), kind=kOutput, calls=%fused_computation | convolution fusion | flops 811597824 | bytes 21069824 | tf_op jit(solution)/shard_map/dot_general | solution.py:27
  171.4 3.5 %low_grads.1 = bf16[2,384,128]{2,1,0:T(8,128)(2,1)} custom-call(bf16[384,256]{1,0:T(8,128)(2,1)} %copy-done.2, bf16[384,256]{1,0:T(8,128)(2,1)} %copy-done.1, bf16[384,128]{1,0:T(8,128)(2,1)} %scatter_kv.1.grad_kv, bf16[3,1344,128]{2,1,0:T(8,128)(2,1)} %get-tuple-element.25.maps), custom_call_target="tpu_custom_call" | custom-call | flops 100000000 | bytes 4000000 | tf_op jit(solution)/shard_map/low_grads/pallas_call | solution.py:544
  174.9 17.0 %sum_tp.3 = bf16[16,48,128]{2,1,0:T(8,128)(2,1)} custom-call(bf16[16,48,128]{2,1,0:T(8,128)(2,1)} %bitcast.27), custom_call_target="tpu_custom_call" | custom-call | flops 3000000000 | bytes 30000000 | tf_op jit(solution)/shard_map/sum_tp/pallas_call | solution.py:184
  191.9 5.5 %block_grads.1 = (bf16[8,1344,128]{2,1,0:T(8,128)(2,1)}, f32[384,512]{1,0:T(8,128)}, f32[384,512]{1,0:T(8,128)}) custom-call(s32[4]{0:T(128)} %pad_add_fusion.1.index_ref, bf16[384,8192]{1,0:T(8,128)(2,1)} %x.3, bf16[384,512]{1,0:T(8,128)(2,1)} %cot.3, bf16[2,384,128]{2,1,0:T(8,128)(2,1)} %bitcast.26, bf16[2,384,128]{2,1,0:T(8,128)(2,1)} %bitcast.28, ...), custom_call_target="tpu_custom_call" | custom-call | flops 1000000000 | bytes 6000000 | tf_op jit(solution)/shard_map/block_grads/pallas_call | solution.py:602
  197.4 4.5 %all-to-all-start.1 = ((bf16[8,1344,128]{2,1,0:T(8,128)(2,1)}), bf16[8,1344,128]{2,1,0:T(8,128)(2,1)}, u32[]{:S(2)}, u32[]{:S(2)}) async-start(bf16[8,1344,128]{2,1,0:T(8,128)(2,1)} %get-tuple-element.35), calls=%async_computation.3 | async-start | bytes 5505024 | tf_op jit(solution)/shard_map/all_to_all | solution.py:799
  201.9 18.1 %reduce-scatter.3.cloned.1.call-done = bf16[384,512]{1,0:T(8,128)(2,1)} async-done(((bf16[384,8192]{1,0:T(8,128)(2,1)}), bf16[384,512]{1,0:T(8,128)(2,1)}) %reduce-scatter.3.cloned.1.call-update) | async-done | bytes 393232 | tf_op jit(solution)/shard_map/reduce_scatter | solution.py:761
  220.1 2.2 add_convert_fusion.2
  222.2 15.4 %all-to-all-done.1.arrived = bf16[8,1344,128]{2,1,0:T(8,128)(2,1)} async-done(((bf16[8,1344,128]{2,1,0:T(8,128)(2,1)}), bf16[8,1344,128]{2,1,0:T(8,128)(2,1)}, u32[]{:S(2)}, u32[]{:S(2)}) %all-to-all-start.1) | async-done | bytes 2752544 | tf_op jit(solution)/shard_map/all_to_all | solution.py:799
  237.7 7.4 %to_store.1 = (f32[4,512,192]{2,1,0:T(8,128)}, f32[4,64,256]{2,1,0:T(8,128)}, f32[4,64,128]{2,1,0:T(8,128)}, f32[4,256,64]{2,1,0:T(8,128)}, f32[4,64,512]{2,1,0:T(8,128)}) custom-call(s32[8]{0:T(128)} %copy-done.13, bf16[8,1344,128]{2,1,0:T(8,128)(2,1)} %all-to-all-done.1.arrived), custom_call_target="tpu_custom_call" | custom-call | bytes 6000000 | tf_op jit(solution)/shard_map/to_store/pallas_call | solution.py:673
  245.1 2.8 copy.30
  247.9 1.9 copy.31
  249.8 61.9 %reduce-scatter.5.cloned.1.call-done = bf16[384,512]{1,0:T(8,128)(2,1)} async-done(((bf16[384,8192]{1,0:T(8,128)(2,1)}), bf16[384,512]{1,0:T(8,128)(2,1)}) %reduce-scatter.5.cloned.1.call-update) | async-done | bytes 393232 | tf_op jit(solution)/shard_map/reduce_scatter | solution.py:781
  311.7 1.9 add_convert_fusion.1
  (52 shorter events, 6.9 us)
Async XLA Ops:
  7.2 23.6 %copy-start = (bf16[8192,128]{1,0:T(8,128)(2,1)S(1)}, bf16[8192,128]{1,0:T(8,128)(2,1)}, u32[]{:S(2)}) copy-start(bf16[8192,128]{1,0:T(8,128)(2,1)} %param.16) | copy-start | bytes 6291460
  7.2 114.6 %all-gather.2.cloned.1.call-start = ((), (), s32[]{:S(2)}) async-start(), calls=%async_computation.5 | async-start | bytes 6684672 | tf_op jit(solution)/shard_map/all_gather | solution.py:751
  12.9 7.4 %copy-start.13 = (s32[8]{0:T(128)}, s32[8]{0:T(128)S(1)}, u32[]{:S(2)}) copy-start(s32[8]{0:T(128)S(1)} %get-tuple-element.62.row_ref) | copy-start | bytes 100
  13.5 12.1 %copy-start.15 = (s32[4]{0:T(128)S(1)}, s32[4]{0:T(128)}, u32[]{:S(2)}) copy-start(s32[4]{0:T(128)} %param.23) | copy-start | bytes 52
  20.4 50.7 %all-to-all-start = ((bf16[8,1344,128]{2,1,0:T(8,128)(2,1)}), bf16[8,1344,128]{2,1,0:T(8,128)(2,1)}, u32[]{:S(2)}, u32[]{:S(2)}) async-start(bf16[8,1344,128]{2,1,0:T(8,128)(2,1)} %serve.1), calls=%async_computation | async-start | bytes 5505024 | tf_op jit(solution)/shard_map/all_to_all | solution.py:748
  25.5 194.5 %reduce-scatter.3.cloned.1.call-start = ((), (), s32[]{:S(2)}) async-start(), calls=%async_computation.4 | async-start | bytes 6684672 | tf_op jit(solution)/shard_map/reduce_scatter | solution.py:761
  30.8 5.4 %copy-start.10 = (bf16[8192,256]{1,0:T(8,128)(2,1)S(1)}, bf16[8192,256]{1,0:T(8,128)(2,1)}, u32[]{:S(2)}) copy-start(bf16[8192,256]{1,0:T(8,128)(2,1)} %param.15) | copy-start | bytes 12582916
  96.7 17.0 %copy-start.5 = (bf16[384,256]{1,0:T(8,128)(2,1)S(1)}, bf16[384,256]{1,0:T(8,128)(2,1)}, u32[]{:S(2)}) copy-start(bf16[384,256]{1,0:T(8,128)(2,1)} %get-tuple-element.26.q_ref) | copy-start | bytes 589828
  113.7 1.4 copy-start.7
  115.1 2.2 copy-start.9
  116.6 12.1 %copy-start.2 = (bf16[384,256]{1,0:T(8,128)(2,1)}, bf16[384,256]{1,0:T(8,128)(2,1)S(1)}, u32[]{:S(2)}) copy-start(bf16[384,256]{1,0:T(8,128)(2,1)S(1)} %get-tuple-element.28.o_ref.attn) | copy-start | bytes 589828
  121.7 1.0 copy-start.14
  121.8 190.0 %reduce-scatter.5.cloned.1.call-start = ((), (), s32[]{:S(2)}) async-start(), calls=%async_computation.6 | async-start | bytes 6684672 | tf_op jit(solution)/shard_map/reduce_scatter | solution.py:781
  122.7 6.0 %copy-start.3 = (f32[384,128]{1,0:T(8,128)S(1)}, f32[384,128]{1,0:T(8,128)}, u32[]{:S(2)}) copy-start(f32[384,128]{1,0:T(8,128)} %get-tuple-element.64.stab) | copy-start | bytes 589828
  122.7 6.0 %copy-start.4 = (f32[384,128]{1,0:T(8,128)S(1)}, f32[384,128]{1,0:T(8,128)}, u32[]{:S(2)}) copy-start(f32[384,128]{1,0:T(8,128)} %get-tuple-element.65.ctab) | copy-start | bytes 589828
  122.7 6.0 %copy-start.8 = (bf16[2,8,384,128]{3,2,1,0:T(8,128)(2,1)S(1)}, bf16[2,8,384,128]{3,2,1,0:T(8,128)(2,1)}, u32[]{:S(2)}) copy-start(bf16[2,8,384,128]{3,2,1,0:T(8,128)(2,1)} %gather_kv.1.kv_ref) | copy-start | bytes 4718596
  131.4 1.1 copy-start.6
  132.5 30.2 %copy-start.1 = (bf16[384,256]{1,0:T(8,128)(2,1)}, bf16[384,256]{1,0:T(8,128)(2,1)S(1)}, u32[]{:S(2)}) copy-start(bf16[384,256]{1,0:T(8,128)(2,1)S(1)} %get-tuple-element.31.grad_q) | copy-start | bytes 589828
  162.8 4.1 %copy-start.11 = (bf16[384,128]{1,0:T(8,128)(2,1)S(1)}, bf16[384,128]{1,0:T(8,128)(2,1)}, u32[]{:S(2)}) copy-start(bf16[384,128]{1,0:T(8,128)(2,1)} %scatter_kv.1.grad_kv) | copy-start | bytes 294916
  197.4 40.2 %all-to-all-start.1 = ((bf16[8,1344,128]{2,1,0:T(8,128)(2,1)}), bf16[8,1344,128]{2,1,0:T(8,128)(2,1)}, u32[]{:S(2)}, u32[]{:S(2)}) async-start(bf16[8,1344,128]{2,1,0:T(8,128)(2,1)} %get-tuple-element.35), calls=%async_computation.3 | async-start | bytes 5505024 | tf_op jit(solution)/shard_map/all_to_all | solution.py:799
  220.1 91.6 %copy-start.12 = (f32[384,512]{1,0:T(8,128)S(1)}, f32[384,512]{1,0:T(8,128)}, u32[]{:S(2)}) copy-start(f32[384,512]{1,0:T(8,128)} %get-tuple-element.34) | copy-start | bytes 2359300
Sparse Core Ops, SparseCore 0:
  10.3 80.8 all-gather.1
  121.9 98.1 reduce-scatter.2
  224.3 87.3 reduce-scatter.4

commit v2 on v1

--- a/solution.py
+++ b/solution.py
@@ -32,13 +32,20 @@
         self.rows = rows
         self.width = width
         self.heads = heads
+        self.cols = heads * HEAD
         self.blocks = rows // BLK
-        self.v = width
-        self.qu = self.v + width // 2
-        self.kvu = self.qu + heads * RANK
-        self.od = self.kvu + RANK
-        self.ou = self.od + HEAD
-        self.total = self.ou + (width // HEAD) * RANK
+        self.dq = slice(0, width)
+        self.dk = slice(width, 2 * width)
+        self.dv = slice(2 * width, 3 * width)
+        at = 3 * width
+        self.qu = slice(at, at + self.cols)
+        at += self.cols
+        self.kvu = slice(at, at + HEAD)
+        at += HEAD
+        self.od = slice(at, at + self.cols)
+        at += self.cols
+        self.ou = slice(at, at + width)
+        self.total = at + width
 
 
 def any_spec():
@@ -54,23 +61,16 @@
 
 
 def serve_body(dim, index_ref, down, q_up, kv_up, o_down, o_up, out):
-    half = dim.width // 2
-    out[0, 0 : dim.width, :] = down[0, :, 0:HEAD]
-    out[0, dim.v : dim.v + half, 0:RANK] = down[0, 0:half, HEAD:]
-    out[0, dim.v : dim.v + half, RANK:] = down[0, half:, HEAD:]
-    for head in range(dim.heads):
-        at = dim.qu + head * RANK
-        out[0, at : at + RANK, :] = q_up[0, :, head * HEAD : (head + 1) * HEAD]
-        out[0, dim.od : dim.od + HEAD, head * RANK : (head + 1) * RANK] = o_down[
-            0, head * HEAD : (head + 1) * HEAD, :
-        ]
-    out[0, dim.kvu : dim.kvu + RANK, :] = kv_up[0]
-    for chunk in range(dim.width // HEAD):
-        at = dim.ou + chunk * RANK
-        out[0, at : at + RANK, :] = o_up[0, :, chunk * HEAD : (chunk + 1) * HEAD]
-
-
-def serve(dim, index, down, q_up, kv_up, o_down, o_up):
+    out[0, :, dim.dq] = down[0, 0:RANK, :]
+    out[0, :, dim.dk] = down[0, RANK : 2 * RANK, :]
+    out[0, :, dim.dv] = down[0, 2 * RANK :, :]
+    out[0, :, dim.qu] = q_up[0]
+    out[0, :, dim.kvu] = kv_up[0]
+    out[0, :, dim.od] = o_down[0]
+    out[0, :, dim.ou] = o_up[0]
+
+
+def serve(dim, index, stores):
     count = index.shape[0]
 
     def picked(array):
@@ -78,30 +78,25 @@
 
     return pl.pallas_call(
         functools.partial(serve_body, dim),
-        out_shape=jax.ShapeDtypeStruct((count, dim.total, HEAD), BF16),
+        out_shape=jax.ShapeDtypeStruct((count, RANK, dim.total), BF16),
         grid_spec=pltpu.PrefetchScalarGridSpec(
             num_scalar_prefetch=1,
             grid=(count,),
-            in_specs=[picked(a) for a in (down, q_up, kv_up, o_down, o_up)],
-            out_specs=pl.BlockSpec((1, dim.total, HEAD), lambda i, idx: (i, 0, 0)),
+            in_specs=[picked(a) for a in stores],
+            out_specs=pl.BlockSpec((1, RANK, dim.total), lambda i, idx: (i, 0, 0)),
         ),
-        cost_estimate=cost(0, 2 * count * dim.total * HEAD * 2),
+        cost_estimate=cost(0, 2 * count * dim.total * RANK * 2),
         name="serve",
-    )(index, down, q_up, kv_up, o_down, o_up)
+    )(index, *stores)
 
 
 def low_parts_body(dim, index_ref, fetched, x, cot, part, maps):
-    half = dim.width // 2
     m = fetched.at[0]
     xb = x[...]
-    part[0] = nn(xb, m[0 : dim.width, :]).astype(BF16)
-    vv = m[dim.v : dim.v + half, :]
-    low_v = nn(xb[:, :half], vv)[:, :RANK] + nn(xb[:, half:], vv)[:, RANK:]
-    low_o = jnp.zeros((BLK, RANK), F32)
-    for chunk in range(dim.width // HEAD):
-        at = dim.ou + chunk * RANK
-        low_o += nt(cot[:, chunk * HEAD : (chunk + 1) * HEAD], m[at : at + RANK, :])
-    part[1] = jnp.concatenate([low_v, low_o], axis=1).astype(BF16)
+    low = [nt(xb, m[:, at]) for at in (dim.dq, dim.dk, dim.dv)]
+    low.append(nt(cot[...], m[:, dim.ou]))
+    part[0] = jnp.concatenate(low[:2], axis=1).astype(BF16)
+    part[1] = jnp.concatenate(low[2:], axis=1).astype(BF16)
     maps[...] = fetched[...]
 
 
@@ -110,22 +105,22 @@
         functools.partial(low_parts_body, dim),
         out_shape=(
             jax.ShapeDtypeStruct((2, dim.rows, HEAD), BF16),
-            jax.ShapeDtypeStruct((dim.blocks, dim.total, HEAD), BF16),
+            jax.ShapeDtypeStruct((dim.blocks, RANK, dim.total), BF16),
         ),
         grid_spec=pltpu.PrefetchScalarGridSpec(
             num_scalar_prefetch=1,
             grid=(dim.blocks,),
             in_specs=[
-                pl.BlockSpec((1, dim.total, HEAD), lambda b, idx: (idx[b], 0, 0)),
+                pl.BlockSpec((1, RANK, dim.total), lambda b, idx: (idx[b], 0, 0)),
                 pl.BlockSpec((BLK, dim.width), lambda b, idx: (b, idx[dim.blocks])),
                 pl.BlockSpec((BLK, dim.width), lambda b, idx: (b, 0)),
             ],
             out_specs=(
                 pl.BlockSpec((2, BLK, HEAD), lambda b, idx: (0, b, 0)),
-                pl.BlockSpec((1, dim.total, HEAD), lambda b, idx: (b, 0, 0)),
+                pl.BlockSpec((1, RANK, dim.total), lambda b, idx: (b, 0, 0)),
             ),
         ),
-        cost_estimate=cost(2 * dim.rows * dim.width * 256, 3 * dim.total * HEAD * 4),
+        cost_estimate=cost(2 * dim.rows * dim.width * 256, 3 * dim.total * RANK * 4),
         name="low_parts",
     )(index, fetched, hidden, cot)
 
@@ -201,6 +196,235 @@
     return out.reshape(shape)
 
 
+def scatter_tp_body(
+    n,
+    parts,
+    by_rows,
+    pair_only,
+    *refs,
+):
+    count = len(parts)
+    lhs = refs[0 : 2 * count : 2]
+    rhs = refs[1 : 2 * count : 2]
+    if pair_only:
+        o_ref, away, cross, own, cross_send, cross_recv = refs[2 * count :]
+    else:
+        (
+            o_ref,
+            away,
+            cross,
+            own,
+            far,
+            near,
+            kept,
+            turn,
+            last,
+            cross_send,
+            cross_recv,
+            far_send,
+            far_recv,
+            near_send,
+            near_recv,
+            last_send,
+            last_recv,
+        ) = refs[2 * count :]
+    width = own.shape[-1]
+    chips = n // 2
+    nz = chips // 2
+    row = lax.axis_index("ctx")
+    me = lax.axis_index("tp")
+    core = lax.rem(me, 2)
+    chip = me // 2
+    z = lax.rem(chip, nz)
+    xh = chip // nz
+    partner = me + 1 - 2 * core
+
+    def device(x_at, z_at):
+        return (x_at * nz + z_at) * 2 + core
+
+    up_z = lax.rem(z + 1, nz)
+    down_z = lax.rem(z + nz - 1, nz)
+    across_z = lax.rem(z + 2, nz)
+    upper = device(xh, up_z)
+    lower = device(xh, down_z)
+    opposite = device(1 - xh, z)
+    barrier = pltpu.get_barrier_semaphore()
+    peers = [partner] if pair_only else [partner, upper, lower, opposite]
+    for peer in peers:
+        pl.semaphore_signal(barrier, inc=1, device_id=(row, peer), device_id_type=MESH)
+    pl.semaphore_wait(barrier, len(peers))
+
+    def product(r, block):
+        rows = pl.ds(r * BLK, BLK)
+        at = pl.ds(pl.multiple_of(block * width, width), width)
+        total = None
+        for a, w in zip(lhs, rhs):
+            term = nt(a[rows, :], w[at, :]) if by_rows else nn(a[rows, :], w[:, at])
+            total = term if total is None else total + term
+        return total.astype(BF16)
+
+    def swap(r, zz, xx):
+        return pltpu.make_async_remote_copy(
+            src_ref=away.at[r, zz, xx],
+            dst_ref=cross.at[r, zz, xx],
+            send_sem=cross_send.at[r, zz, xx],
+            recv_sem=cross_recv.at[r, zz, xx],
+            device_id=(row, partner),
+            device_id_type=MESH,
+        )
+
+    def places(step):
+        zz = lax.rem(z + jnp.where(step < 2, 2, jnp.where(step < 4, 1, jnp.where(step < 6, nz - 1, 0))), nz)
+        return zz, lax.rem(step, 2)
+
+    def multiply(r):
+        def one(step, carry):
+            zz, xx = places(step)
+            chip_at = xx * nz + zz
+            away[r, zz, xx] = product(r, chip_at * 2 + 1 - core)
+            swap(r, zz, xx).start()
+            own[r, zz, xx] = product(r, chip_at * 2 + core)
+            return carry
+
+        lax.fori_loop(0, chips, one, 0)
+
+    def join(r, zz, rows=slice(0, BLK)):
+        for xx in range(2):
+            swap(r, zz, xx).wait_recv()
+            own[r, zz, xx] = (own[r, zz, xx].astype(F32) + cross[r, zz, xx].astype(F32)).astype(BF16)
+
+    half = (slice(0, BLK // 2), slice(BLK // 2, BLK))
+
+    def far_copy(r, way):
+        return pltpu.make_async_remote_copy(
+            src_ref=own.at[r, across_z, :, half[way], :],
+            dst_ref=far.at[r, way],
+            send_sem=far_send.at[r, way],
+            recv_sem=far_recv.at[r, way],
+            device_id=(row, upper if way == 0 else lower),
+            device_id_type=MESH,
+        )
+
+    def near_copy(r, way):
+        return pltpu.make_async_remote_copy(
+            src_ref=own.at[r, up_z if way == 0 else down_z],
+            dst_ref=near.at[r, way],
+            send_sem=near_send.at[r, way],
+            recv_sem=near_recv.at[r, way],
+            device_id=(row, upper if way == 0 else lower),
+            device_id_type=MESH,
+        )
+
+    def last_copy(r):
+        return pltpu.make_async_remote_copy(
+            src_ref=turn.at[r],
+            dst_ref=last.at[r],
+            send_sem=last_send.at[r],
+            recv_sem=last_recv.at[r],
+            device_id=(row, opposite),
+            device_id_type=MESH,
+        )
+
+    def stage_far(r):
+        join(r, across_z)
+        for way in range(2):
+            far_copy(r, way).start()
+        for zz in (up_z, down_z, z):
+            join(r, zz)
+
+    def stage_near(r):
+        for way in range(2):
+            far_copy(r, way).wait_recv()
+            zz = up_z if way == 0 else down_z
+            own[r, zz, :, half[way], :] = (
+                own[r, zz, :, half[way], :].astype(F32) + far[r, way].astype(F32)
+            ).astype(BF16)
+            near_copy(r, way).start()
+
+    def stage_last(r):
+        for way in range(2):
+            near_copy(r, way).wait_recv()
+        for other in range(2):
+            xx = xh if other == 0 else 1 - xh
+            total = (
+                own[r, z, xx].astype(F32)
+                + near[r, 0, xx].astype(F32)
+                + near[r, 1, xx].astype(F32)
+            )
+            if other == 0:
+                kept[r] = total
+            else:
+                turn[r] = total.astype(BF16)
+        last_copy(r).start()
+
+    def finish(r):
+        last_copy(r).wait_recv()
+        o_ref[pl.ds(r * BLK, BLK), :] = kept[r] + last[r].astype(F32)
+
+    chunks = own.shape[0]
+    if pair_only:
+        for r in range(chunks + 1):
+            if r < chunks:
+                multiply(r)
+            if r >= 1:
+                for zz in range(nz):
+                    join(r - 1, zz)
+                    for xx in range(2):
+                        o_ref[xx * nz + zz, pl.ds((r - 1) * BLK, BLK), :] = own[r - 1, zz, xx]
+    else:
+        stages = (multiply, stage_far, stage_near, stage_last, finish)
+        for tick in range(chunks + len(stages) - 1):
+            for depth in reversed(range(len(stages))):
+                if 0 <= tick - depth < chunks:
+                    stages[depth](tick - depth)
+    for r in range(chunks):
+        for zz in range(nz):
+            for xx in range(2):
+                swap(r, zz, xx).wait_send()
+        if not pair_only:
+            for way in range(2):
+                far_copy(r, way).wait_send()
+                near_copy(r, way).wait_send()
+            last_copy(r).wait_send()
+
+
+def scatter_tp(parts, by_rows, pair_only, width, collective_id):
+    n = lax.axis_size("tp")
+    chips = n // 2
+    nz = chips // 2
+    rows = parts[0][0].shape[0]
+    chunks = rows // BLK
+    sems = pltpu.SemaphoreType.DMA
+    big = pltpu.VMEM((chunks, nz, 2, BLK, width), BF16)
+    scratch = [big, big, big]
+    sem_shapes = [sems((chunks, nz, 2))] * 2
+    if pair_only:
+        out_shape = jax.ShapeDtypeStruct((chips, rows, width), BF16)
+    else:
+        out_shape = jax.ShapeDtypeStruct((rows, width), F32)
+        scratch += [
+            pltpu.VMEM((chunks, 2, 2, BLK // 2, width), BF16),
+            pltpu.VMEM((chunks, 2, 2, BLK, width), BF16),
+            pltpu.VMEM((chunks, BLK, width), F32),
+            pltpu.VMEM((chunks, BLK, width), BF16),
+            pltpu.VMEM((chunks, BLK, width), BF16),
+        ]
+        sem_shapes += [sems((chunks, 2))] * 4 + [sems((chunks,))] * 2
+    flat = [x for pair in parts for x in pair]
+    return pl.pallas_call(
+        functools.partial(scatter_tp_body, n, parts, by_rows, pair_only),
+        out_shape=out_shape,
+        in_specs=[vmem_spec()] * len(flat),
+        out_specs=vmem_spec(),
+        scratch_shapes=scratch + sem_shapes,
+        compiler_params=pltpu.CompilerParams(
+            collective_id=collective_id, has_side_effects=True, vmem_limit_bytes=44 << 20
+        ),
+        cost_estimate=cost(3e10, 1e8),
+        name="pair_tp" if pair_only else "scatter_tp",
+    )(*flat)
+
+
 def finalize_body(dim, xq, xkv, low, maps, ctab, stab, q_out, kv_out, delta_out):
     core = lax.rem(lax.axis_index("tp"), 2)
     is_value = core == 1
@@ -214,14 +438,13 @@
         low_o = second[:, RANK:]
         cosine = ctab[rows, :]
         sine = stab[rows, :]
+        delta_out[rows, :] = nn(low_o, m[:, dim.od])
+        turn = xq[rows, :] + nn(low_q, m[:, dim.qu])
         for head in range(dim.heads):
             cols = slice(head * HEAD, (head + 1) * HEAD)
-            at = dim.qu + head * RANK
-            q = xq[rows, cols] + nn(low_q, m[at : at + RANK, :])
+            q = turn[:, cols]
             q_out[rows, cols] = (q * cosine + pltpu.roll(q, HEAD // 2, 1) * sine).astype(BF16)
-            lane = slice(head * RANK, (head + 1) * RANK)
-            delta_out[rows, cols] = nt(low_o, m[dim.od : dim.od + HEAD, lane])
-        kv = xkv[rows, :] + nn(low_kv, m[dim.kvu : dim.kvu + RANK, :])
+        kv = xkv[rows, :] + nn(low_kv, m[:, dim.kvu])
         kv = kv.astype(BF16).astype(F32)
         turned = kv * cosine + pltpu.roll(kv, HEAD // 2, 1) * sine
         kv_out[rows, :] = jnp.where(is_value, kv, turned).astype(BF16)
@@ -523,15 +746,9 @@
 def low_grads_body(dim, attn, grad_q, grad_kv, maps, part):
     core = lax.rem(lax.axis_index("tp"), 2)
     m = maps.at[0]
-    low_q = jnp.zeros((BLK, RANK), F32)
-    low_out = jnp.zeros((BLK, RANK), F32)
-    for head in range(dim.heads):
-        cols = slice(head * HEAD, (head + 1) * HEAD)
-        lane = slice(head * RANK, (head + 1) * RANK)
-        at = dim.qu + head * RANK
-        low_q += nt(grad_q[:, cols], m[at : at + RANK, :])
-        low_out += nn(attn[:, cols], m[dim.od : dim.od + HEAD, lane])
-    low_kv = nt(grad_kv[...], m[dim.kvu : dim.kvu + RANK, :])
+    low_q = nt(grad_q[...], m[:, dim.qu])
+    low_out = nt(attn[...], m[:, dim.od])
+    low_kv = nt(grad_kv[...], m[:, dim.kvu])
     zero = jnp.zeros_like(low_kv)
     low_k = jnp.where(core == 0, low_kv, zero)
     low_v = jnp.where(core == 1, low_kv, zero)
@@ -549,7 +766,7 @@
             pl.BlockSpec((BLK, cols), lambda b: (b, 0)),
             pl.BlockSpec((BLK, cols), lambda b: (b, 0)),
             pl.BlockSpec((BLK, HEAD), lambda b: (b, 0)),
-            pl.BlockSpec((1, dim.total, HEAD), lambda b: (b, 0, 0)),
+            pl.BlockSpec((1, RANK, dim.total), lambda b: (b, 0, 0)),
         ],
         out_specs=pl.BlockSpec((2, BLK, HEAD), lambda b: (0, b, 0)),
         cost_estimate=cost(1e8, 4e6),
@@ -560,39 +777,27 @@
 def block_grads_body(
     dim, index_ref, x, cot, low_in, low_grad, attn, grad_q, grad_kv, maps, out, d_in, d_out
 ):
-    half = dim.width // 2
     core = lax.rem(lax.axis_index("tp"), 2)
     m = maps.at[0]
-    low_qk_t = low_in[0].T
-    low_vo_t = low_in[1].T
-    low_q_t = low_qk_t[:RANK]
-    low_kv_t = jnp.where(core == 1, low_vo_t[:RANK], low_qk_t[RANK:])
-    low_o = low_in[1, :, RANK:]
-    g_qk = low_grad[0]
-    g_v = low_grad[1, :, :RANK]
-    low_out = low_grad[1, :, RANK:]
-    low_out_t = low_out.T
-    xt = x[...].T
-    out[0, 0 : dim.width, :] = nn(xt, g_qk).astype(BF16)
-    up = nn(xt, g_v).astype(BF16)
-    out[0, dim.v : dim.v + half, 0:RANK] = up[:half]
-    out[0, dim.v : dim.v + half, RANK:] = up[half:]
-    for head in range(dim.heads):
-        cols = slice(head * HEAD, (head + 1) * HEAD)
-        lane = slice(head * RANK, (head + 1) * RANK)
-        at = dim.qu + head * RANK
-        out[0, at : at + RANK, :] = nn(low_q_t, grad_q[:, cols]).astype(BF16)
-        out[0, dim.od : dim.od + HEAD, lane] = nn(attn[:, cols].T, low_o).astype(BF16)
-    out[0, dim.kvu : dim.kvu + RANK, :] = nn(low_kv_t, grad_kv[...]).astype(BF16)
-    for chunk in range(dim.width // HEAD):
-        cols = slice(chunk * HEAD, (chunk + 1) * HEAD)
-        at = dim.ou + chunk * RANK
-        out[0, at : at + RANK, :] = nn(low_out_t, cot[:, cols]).astype(BF16)
-        d_out[:, cols] = nn(low_out, m[at : at + RANK, :])
-    vv = m[dim.v : dim.v + half, :]
-    d_qk = nt(g_qk, m[0 : dim.width, :])
-    d_in[:, :half] = d_qk[:, :half] + nt(g_v, vv[:, :RANK])
-    d_in[:, half:] = d_qk[:, half:] + nt(g_v, vv[:, RANK:])
+    first_t = low_in[0].T
+    second_t = low_in[1].T
+    low_kv_t = jnp.where(core == 1, second_t[:RANK], first_t[RANK:])
+    g_qk_t = low_grad[0].T
+    g_vo_t = low_grad[1].T
+    xb = x[...]
+    out[0, :, dim.dq] = nn(g_qk_t[:RANK], xb).astype(BF16)
+    out[0, :, dim.dk] = nn(g_qk_t[RANK:], xb).astype(BF16)
+    out[0, :, dim.dv] = nn(g_vo_t[:RANK], xb).astype(BF16)
+    out[0, :, dim.qu] = nn(first_t[:RANK], grad_q[...]).astype(BF16)
+    out[0, :, dim.kvu] = nn(low_kv_t, grad_kv[...]).astype(BF16)
+    out[0, :, dim.od] = nn(second_t[RANK:], attn[...]).astype(BF16)
+    out[0, :, dim.ou] = nn(g_vo_t[RANK:], cot[...]).astype(BF16)
+    d_out[...] = nn(low_grad[1, :, RANK:], m[:, dim.ou])
+    d_in[...] = (
+        nn(low_grad[0, :, :RANK], m[:, dim.dq])
+        + nn(low_grad[0, :, RANK:], m[:, dim.dk])
+        + nn(low_grad[1, :, :RANK], m[:, dim.dv])
+    )
 
 
 def block_grads(dim, index, owners, hidden, cot, low_in, low_grad, attn, grad_q, grad_kv, maps):
@@ -602,7 +807,7 @@
     return pl.pallas_call(
         functools.partial(block_grads_body, dim),
         out_shape=(
-            jax.ShapeDtypeStruct((owners, dim.total, HEAD), BF16),
+            jax.ShapeDtypeStruct((owners, RANK, dim.total), BF16),
             jax.ShapeDtypeStruct((dim.rows, dim.width), F32),
             jax.ShapeDtypeStruct((dim.rows, dim.width), F32),
         ),
@@ -617,10 +822,10 @@
                 pl.BlockSpec((BLK, cols), lambda b, idx: (b, 0)),
                 pl.BlockSpec((BLK, cols), lambda b, idx: (b, 0)),
                 pl.BlockSpec((BLK, HEAD), lambda b, idx: (b, 0)),
-                pl.BlockSpec((1, dim.total, HEAD), lambda b, idx: (b, 0, 0)),
+                pl.BlockSpec((1, RANK, dim.total), lambda b, idx: (b, 0, 0)),
             ],
             out_specs=(
-                pl.BlockSpec((1, dim.total, HEAD), lambda b, idx: (idx[b], 0, 0)),
+                pl.BlockSpec((1, RANK, dim.total), lambda b, idx: (idx[b], 0, 0)),
                 wide_spec,
                 wide_spec,
             ),
@@ -630,55 +835,44 @@
     )(index, hidden, cot, low_in, low_grad, attn, grad_q, grad_kv, maps)
 
 
-def store_body(dim, count, row_ref, arrived, down, q_up, kv_up, o_down, o_up, acc):
-    half = dim.width // 2
+def store_body(dim, row_ref, arrived, down, q_up, kv_up, o_down, o_up):
     i = pl.program_id(0)
 
     @pl.when(i == 0)
     def _():
-        acc[...] = jnp.zeros_like(acc)
+        for ref in (down, q_up, kv_up, o_down, o_up):
+            ref[...] = jnp.zeros_like(ref)
 
     row = row_ref[i]
 
     @pl.when(row >= 0)
     def _():
-        acc[row] += arrived[0].astype(F32)
-
-    @pl.when(i == count - 1)
-    def _():
-        for s in range(acc.shape[0]):
-            down[s, :, 0:HEAD] = acc[s, 0 : dim.width, :]
-            down[s, :half, HEAD:] = acc[s, dim.v : dim.v + half, :RANK]
-            down[s, half:, HEAD:] = acc[s, dim.v : dim.v + half, RANK:]
-            for head in range(dim.heads):
-                cols = slice(head * HEAD, (head + 1) * HEAD)
-                at = dim.qu + head * RANK
-                q_up[s, :, cols] = acc[s, at : at + RANK, :]
-                o_down[s, cols, :] = acc[
-                    s, dim.od : dim.od + HEAD, head * RANK : (head + 1) * RANK
-                ]
-            kv_up[s] = acc[s, dim.kvu : dim.kvu + RANK, :]
-            for chunk in range(dim.width // HEAD):
-                at = dim.ou + chunk * RANK
-                o_up[s, :, chunk * HEAD : (chunk + 1) * HEAD] = acc[s, at : at + RANK, :]
+        def piece(at):
+            return arrived[0, :, at].astype(F32)
+
+        down[row, 0:RANK, :] += piece(dim.dq)
+        down[row, RANK : 2 * RANK, :] += piece(dim.dk)
+        down[row, 2 * RANK :, :] += piece(dim.dv)
+        q_up[row] += piece(dim.qu)
+        kv_up[row] += piece(dim.kvu)
+        o_down[row] += piece(dim.od)
+        o_up[row] += piece(dim.ou)
 
 
 def to_store(dim, rows, arrived, shapes):
     count = arrived.shape[0]
-    tenants = shapes[0][0]
 
     def whole(shape):
         return pl.BlockSpec(shape, lambda i, idx: (0, 0, 0))
 
     return pl.pallas_call(
-        functools.partial(store_body, dim, count),
+        functools.partial(store_body, dim),
         out_shape=tuple(jax.ShapeDtypeStruct(s, F32) for s in shapes),
         grid_spec=pltpu.PrefetchScalarGridSpec(
             num_scalar_prefetch=1,
             grid=(count,),
-            in_specs=[pl.BlockSpec((1, dim.total, HEAD), lambda i, idx: (i, 0, 0))],
+            in_specs=[pl.BlockSpec((1, RANK, dim.total), lambda i, idx: (i, 0, 0))],
             out_specs=tuple(whole(s) for s in shapes),
-            scratch_shapes=[pltpu.VMEM((tenants, dim.total, HEAD), F32)],
         ),
         cost_estimate=cost(0, 6e6),
         name="to_store",
@@ -708,10 +902,10 @@
     tenants = adapter_qkv_down_store.shape[0]
     dim = Dims(rows_dev, out_cols, query_projection.shape[1] // HEAD)
     stores = (
-        adapter_qkv_down_store,
+        jnp.swapaxes(adapter_qkv_down_store, 1, 2),
         adapter_query_up,
         adapter_key_value_up,
-        adapter_output_down,
+        jnp.swapaxes(adapter_output_down, 1, 2),
         adapter_output_up,
     )
 
@@ -746,7 +940,7 @@
     stab = jnp.sin(angles) * sign[None, :]
 
     fetched = lax.all_to_all(
-        serve(dim, serve_index, *stores), "ctx", split_axis=0, concat_axis=0, tiled=True
+        serve(dim, serve_index, stores), "ctx", split_axis=0, concat_axis=0, tiled=True
     )
     pieces = lax.all_gather(output_cotangent, "tp", axis=1, tiled=True)
     xq = jnp.dot(hidden_input, query_projection, preferred_element_type=F32)
@@ -758,12 +952,12 @@
     kv_all = gather_kv(keyval, 1)
     attn, lse = attend(dim, meta, start, query, kv_all)
 
+    tp_count = lax.axis_size("tp")
+    groups = [[2 * i + core for i in range(tp_count // 2)] for core in range(2)]
+    paired = scatter_tp(((attn, output_projection),), False, True, out_cols, 4)
     heads_total = lax.psum_scatter(
-        jnp.dot(attn, output_projection, preferred_element_type=F32).astype(BF16),
-        "tp",
-        scatter_dimension=1,
-        tiled=True,
-    ).astype(F32)
+        paired, "tp", scatter_dimension=0, axis_index_groups=groups, tiled=True
+    )[0].astype(F32)
 
     grad_attn = (
         lax.dot_general(
@@ -777,10 +971,6 @@
     grad_kv = scatter_kv(grad_kv_all, ctab, stab, 2)
 
     low_grad = sum_tp(low_grads(dim, attn, grad_q, grad_kv, maps), 0)
-    input_part = nt(grad_q, query_projection) + nt(grad_kv, key_value_projection)
-    input_total = lax.psum_scatter(
-        input_part.astype(BF16), "tp", scatter_dimension=1, tiled=True
-    ).astype(F32)
     sent, d_in, d_out = block_grads(
         dim,
         pick_index,
@@ -794,11 +984,27 @@
         grad_kv,
         maps,
     )
+    grad_q_late, grad_kv_late, sent = lax.optimization_barrier((grad_q, grad_kv, sent))
+    input_total = scatter_tp(
+        ((grad_q_late, query_projection), (grad_kv_late, key_value_projection)),
+        True,
+        False,
+        out_cols,
+        3,
+    )
     output = (heads_total + d_out).astype(BF16)
     hidden_input_gradient = (input_total + d_in).astype(BF16)
     returned = lax.all_to_all(sent, "ctx", split_axis=0, concat_axis=0, tiled=True)
     grads = to_store(dim, served_row, returned, [s.shape for s in stores])
-    return (output, hidden_input_gradient) + tuple(grads)
+    return (
+        output,
+        hidden_input_gradient,
+        jnp.swapaxes(grads[0], 1, 2),
+        grads[1],
+        grads[2],
+        jnp.swapaxes(grads[3], 1, 2),
+        grads[4],
+    )
 
 
 def solution(mesh):

time: 321 us -> 283 us (0.88)
  waiting for transfers between devices: 126 us -> 48 us
  Pallas kernels: 117 us -> 176 us
  matrix products: 29.7 us -> 16.7 us
  local copies, waits for them, and re-layouts: 13 us -> 6.24 us
    reduce_scatter x2 -> x1, waiting for transfers between devices: 80.1 us -> 20 us  [body(): lax.psum_scatter(paired, 'tp', scatter_dimension=0, axis_index_groups=gro...]
    pallas_call x1 -> x3, Pallas kernels: 7.42 us -> 66.4 us  [the longest x2 59.8 us: scatter_tp(): pl.pallas_call(functools.partial(scatter_tp_body, n, parts, by_rows, pair...]
    all_to_all x1, waiting for transfers between devices: 15.4 us -> 0.01 us  [body(): lax.all_to_all(sent, 'ctx', split_axis=0, concat_axis=0, tiled=True)]
    dot_general x3 -> x0, matrix products: 13 us -> none  [the longest x2 8.57 us: nt(): lax.dot_general(a, b, (((1,), (1,)), ((), ())), preferred_element_type=F32)]
    unnamed x36 -> x38, local copies, waits for them, and re-layouts: 12.9 us -> 6.15 us
  transfers between devices with their start and end apart: 5 -> 4, of which waited for: 4 -> 2; matrix products, arithmetic and copies ran while one was open for 14% -> 9% of each run, Pallas kernels for 37% -> 60%
where the time goes in v2:
time: 283 us; the launch traced here: 282 us
  Pallas kernels  176 us (62%)
  waiting for transfers between devices  48 us (17%)
  between operations  17.7 us (6%)
  matrix products  16.7 us (6%)
  starting transfers between devices  10.6 us (4%)
  other arithmetic  7.44 us (3%)
  local copies, waits for them, and re-layouts  6.24 us (2%)
    pallas_call x2, Pallas kernels, scatter_tp(): pl.pallas_call(functools.partial(scatter_tp_body, n, parts, by_rows, pair...  59.8 us
    pallas_call x2, Pallas kernels, sum_tp(): pl.pallas_call(functools.partial(sum_tp_body, n), out_shape=jax.ShapeDtyp...  35.9 us
    pallas_call x1, Pallas kernels, scatter_kv(): pl.pallas_call(functools.partial(scatter_kv_body, n), out_shape=jax.Shape...  30.6 us
    all_to_all x1, waiting for transfers between devices, body(): lax.all_to_all(serve(dim, serve_index, stores), 'ctx', split_axis=0, conc...  27.3 us
    reduce_scatter x1, waiting for transfers between devices, body(): lax.psum_scatter(paired, 'tp', scatter_dimension=0, axis_index_groups=gro...  20 us
    pallas_call x1, Pallas kernels, gather_kv(): pl.pallas_call(functools.partial(gather_kv_body, n), out_shape=jax.ShapeD...  16.7 us
    pallas_call x1, Pallas kernels, to_store(): pl.pallas_call(functools.partial(store_body, dim), out_shape=tuple((jax.S...  6.6 us
    unnamed x38, local copies, waits for them, and re-layouts  6.15 us
  transfers between devices with their start and end apart: 4, of which 2 were waited for; matrix products, arithmetic and copies ran while one was open for 9% of the time, Pallas kernels for 60%

profile of v2, /device:TPU:0, one launch (start us, length us, event | category | flops | bytes accessed | tf_op | source)
XLA Modules:
  0.0 282.5 jit_solution(1526887923878179331)
XLA Ops:
  8.0 0.7 all-gather.2.cloned.1.call-update
  8.7 0.9 select_reduce_fusion
  10.3 6.0 %serve.1 = bf16[8,64,2688]{2,1,0:T(8,128)(2,1)} custom-call(s32[8]{0:T(128)} %broadcast_maximum_fusion.index_ref, bf16[4,192,512]{2,1,0:T(8,128)(2,1)} %bitcast.26, bf16[4,64,256]{2,1,0:T(8,128)(2,1)} %q_up.1, bf16[4,64,128]{2,1,0:T(8,128)(2,1)} %kv_up.1, bf16[4,64,256]{2,1,0:T(8,128)(2,1)} %bitcast.31, bf16[4,64,512]{2,1,0:T(8,128)(2,1)} %o_up.1), custom_call_target="tpu_custom_call" | custom-call | bytes 5505024 | tf_op jit(solution)/shard_map/serve/pallas_call | solution.py:79
  16.3 6.0 %all-to-all-start = ((bf16[8,64,2688]{2,1,0:T(8,128)(2,1)}), bf16[8,64,2688]{2,1,0:T(8,128)(2,1)}, u32[]{:S(2)}, u32[]{:S(2)}) async-start(bf16[8,64,2688]{2,1,0:T(8,128)(2,1)} %serve.1), calls=%async_computation | async-start | bytes 5505024 | tf_op jit(solution)/shard_map/all_to_all | solution.py:942
  25.3 0.7 pad_add_fusion.1.index_ref
  26.1 1.5 fusion.2
  27.6 5.4 %fusion.8.xkv = f32[384,128]{1,0:T(8,128)} fusion(bf16[384,8192]{1,0:T(8,128)(2,1)} %x.3, bf16[8192,128]{1,0:T(8,128)(2,1)S(1)} %copy-done), kind=kOutput, calls=%fused_computation.31 | convolution fusion | flops 805306368 | bytes 8585216 | tf_op jit(solution)/shard_map/dot_general | solution.py:947
  33.0 5.4 %fusion.7.xq = f32[384,256]{1,0:T(8,128)} fusion(bf16[384,8192]{1,0:T(8,128)(2,1)} %x.3, bf16[8192,256]{1,0:T(8,128)(2,1)S(1)} %copy-done.8), kind=kOutput, calls=%fused_computation.30 | convolution fusion | flops 1610612736 | bytes 10878976 | tf_op jit(solution)/shard_map/dot_general | solution.py:946
  38.3 27.3 %all-to-all-done.fetched = bf16[8,64,2688]{2,1,0:T(8,128)(2,1)} async-done(((bf16[8,64,2688]{2,1,0:T(8,128)(2,1)}), bf16[8,64,2688]{2,1,0:T(8,128)(2,1)}, u32[]{:S(2)}, u32[]{:S(2)}) %all-to-all-start) | async-done | bytes 2752544 | tf_op jit(solution)/shard_map/all_to_all | solution.py:942
  65.6 4.5 %low_parts.1 = (bf16[2,384,128]{2,1,0:T(8,128)(2,1)}, bf16[3,64,2688]{2,1,0:T(8,128)(2,1)}) custom-call(s32[4]{0:T(128)} %pad_add_fusion.1.index_ref, bf16[8,64,2688]{2,1,0:T(8,128)(2,1)} %all-to-all-done.fetched, bf16[384,8192]{1,0:T(8,128)(2,1)} %x.3, bf16[384,512]{1,0:T(8,128)(2,1)} %cot.3), custom_call_target="tpu_custom_call" | custom-call | flops 100663296 | bytes 2064384 | tf_op jit(solution)/shard_map/low_parts/pallas_call | solution.py:104
  70.1 19.7 %sum_tp.2 = bf16[16,48,128]{2,1,0:T(8,128)(2,1)} custom-call(bf16[16,48,128]{2,1,0:T(8,128)(2,1)} %bitcast.35), custom_call_target="tpu_custom_call" | custom-call | flops 3000000000 | bytes 30000000 | tf_op jit(solution)/shard_map/sum_tp/pallas_call | solution.py:179
  89.8 2.8 %finalize.1 = (bf16[384,256]{1,0:T(8,128)(2,1)}, bf16[384,128]{1,0:T(8,128)(2,1)}, f32[384,256]{1,0:T(8,128)}) custom-call(f32[384,256]{1,0:T(8,128)} %fusion.7.xq, f32[384,128]{1,0:T(8,128)} %fusion.8.xkv, bf16[2,384,128]{2,1,0:T(8,128)(2,1)} %bitcast.27, bf16[3,64,2688]{2,1,0:T(8,128)(2,1)} %get-tuple-element.28.maps, f32[384,128]{1,0:T(8,128)} %get-tuple-element.50.ctab, ...), custom_call_target="tpu_custom_call" | custom-call | flops 100000000 | bytes 4000000 | tf_op jit(solution)/shard_map/finalize/pallas_call | solution.py:455
  92.6 16.7 %gather_kv.1.kv_ref = bf16[2,8,384,128]{3,2,1,0:T(8,128)(2,1)} custom-call(bf16[384,128]{1,0:T(8,128)(2,1)} %get-tuple-element.30.x_ref), custom_call_target="tpu_custom_call" | custom-call | flops 3000000000 | bytes 30000000 | tf_op jit(solution)/shard_map/gather_kv/pallas_call | solution.py:525
  109.4 1.4 copy-done.12
  110.8 1.5 attend.1
  112.3 0.7 copy-done.7
  113.0 13.5 %pair_tp.1 = bf16[8,384,512]{2,1,0:T(8,128)(2,1)} custom-call(bf16[384,256]{1,0:T(8,128)(2,1)S(1)} %get-tuple-element.31.refs_0_.o_ref.attn, bf16[256,8192]{1,0:T(8,128)(2,1)S(1)} %copy-done.7), custom_call_target="tpu_custom_call" | custom-call | flops 30000001024 | bytes 100000000 | tf_op jit(solution)/shard_map/pair_tp/pallas_call | solution.py:414
  126.5 6.0 %fusion.do_ref = bf16[384,256]{1,0:T(8,128)(2,1)S(1)} fusion(f32[384,256]{1,0:T(8,128)S(1)} %copy-done.17, bf16[384,8192]{1,0:T(8,128)(2,1)} %all-gather.2.cloned.1.call-done, bf16[256,8192]{1,0:T(8,128)(2,1)} %refs_1_.2), kind=kOutput, calls=%fused_computation.1 | convolution fusion | flops 1610809344 | bytes 11075584 | tf_op jit(solution)/shard_map/dot_general | solution.py:963
  132.5 2.6 attend_back.1
  135.2 0.7 copy-done.4
  135.9 1.1 copy-done.11
  137.0 30.6 %scatter_kv.1.grad_kv.refs_2_ = bf16[384,128]{1,0:T(8,128)(2,1)} custom-call(bf16[2,8,384,128]{3,2,1,0:T(8,128)(2,1)} %copy-done.11, f32[384,128]{1,0:T(8,128)} %get-tuple-element.50.ctab, f32[384,128]{1,0:T(8,128)} %get-tuple-element.49.stab), custom_call_target="tpu_custom_call" | custom-call | flops 3000000000 | bytes 30000000 | tf_op jit(solution)/shard_map/scatter_kv/pallas_call | solution.py:729
  167.6 3.4 %low_grads.1 = bf16[2,384,128]{2,1,0:T(8,128)(2,1)} custom-call(bf16[384,256]{1,0:T(8,128)(2,1)} %copy-done.3, bf16[384,256]{1,0:T(8,128)(2,1)} %copy-done.4, bf16[384,128]{1,0:T(8,128)(2,1)} %scatter_kv.1.grad_kv.refs_2_, bf16[3,64,2688]{2,1,0:T(8,128)(2,1)} %get-tuple-element.28.maps), custom_call_target="tpu_custom_call" | custom-call | flops 100000000 | bytes 4000000 | tf_op jit(solution)/shard_map/low_grads/pallas_call | solution.py:761
  171.0 16.3 %sum_tp.3 = bf16[16,48,128]{2,1,0:T(8,128)(2,1)} custom-call(bf16[16,48,128]{2,1,0:T(8,128)(2,1)} %bitcast.29), custom_call_target="tpu_custom_call" | custom-call | flops 3000000000 | bytes 30000000 | tf_op jit(solution)/shard_map/sum_tp/pallas_call | solution.py:179
  187.2 5.4 %block_grads.1 = (bf16[8,64,2688]{2,1,0:T(8,128)(2,1)}, f32[384,512]{1,0:T(8,128)}, f32[384,512]{1,0:T(8,128)}) custom-call(s32[4]{0:T(128)} %pad_add_fusion.1.index_ref, bf16[384,8192]{1,0:T(8,128)(2,1)} %x.3, bf16[384,512]{1,0:T(8,128)(2,1)} %cot.3, bf16[2,384,128]{2,1,0:T(8,128)(2,1)} %bitcast.28, bf16[2,384,128]{2,1,0:T(8,128)(2,1)} %bitcast.30, ...), custom_call_target="tpu_custom_call" | custom-call | flops 1000000000 | bytes 6000000 | tf_op jit(solution)/shard_map/block_grads/pallas_call | solution.py:807
  192.6 4.6 %all-to-all-start.1 = ((bf16[8,64,2688]{2,1,0:T(8,128)(2,1)}), bf16[8,64,2688]{2,1,0:T(8,128)(2,1)}, u32[]{:S(2)}, u32[]{:S(2)}) async-start(bf16[8,64,2688]{2,1,0:T(8,128)(2,1)} %get-tuple-element.41), calls=%async_computation.2 | async-start | bytes 5505024 | tf_op jit(solution)/shard_map/all_to_all | solution.py:997
  197.2 20.0 %reduce-scatter.2.cloned.1.call-done = bf16[1,384,512]{2,1,0:T(8,128)(2,1)} async-done(((bf16[8,384,512]{2,1,0:T(8,128)(2,1)}), bf16[1,384,512]{2,1,0:T(8,128)(2,1)}) %reduce-scatter.2.cloned.1.call-update) | async-done | bytes 393232 | tf_op jit(solution)/shard_map/reduce_scatter | solution.py:958
  217.1 1.9 fusion.1
  219.0 2.2 copy-done.9
  221.2 46.4 %scatter_tp.1 = f32[384,512]{1,0:T(8,128)S(1)} custom-call(bf16[384,256]{1,0:T(8,128)(2,1)S(1)} %copy-done.5, bf16[8192,256]{1,0:T(8,128)(2,1)S(1)} %copy-done.9, bf16[384,128]{1,0:T(8,128)(2,1)S(1)} %copy-done.6, bf16[8192,128]{1,0:T(8,128)(2,1)S(1)} %copy-done), custom_call_target="tpu_custom_call" | custom-call | flops 30000001024 | bytes 100000000 | tf_op jit(solution)/shard_map/scatter_tp/pallas_call | solution.py:414
  267.6 0.9 add_convert_fusion
  268.4 6.6 %to_store.1 = (f32[4,192,512]{2,1,0:T(8,128)}, f32[4,64,256]{2,1,0:T(8,128)}, f32[4,64,128]{2,1,0:T(8,128)}, f32[4,64,256]{2,1,0:T(8,128)}, f32[4,64,512]{2,1,0:T(8,128)}) custom-call(s32[8]{0:T(128)} %copy-done.16, bf16[8,64,2688]{2,1,0:T(8,128)(2,1)} %all-to-all-done.1.arrived), custom_call_target="tpu_custom_call" | custom-call | bytes 6000000 | tf_op jit(solution)/shard_map/to_store/pallas_call | solution.py:868
  (50 shorter events, 2.0 us)
Async XLA Ops:
  8.0 118.5 %all-gather.2.cloned.1.call-start = ((), (), s32[]{:S(2)}) async-start(), calls=%async_computation.4 | async-start | bytes 6684672 | tf_op jit(solution)/shard_map/all_gather | solution.py:945
  9.8 6.5 %copy-start.16 = (s32[8]{0:T(128)}, s32[8]{0:T(128)S(1)}, u32[]{:S(2)}) copy-start(s32[8]{0:T(128)S(1)} %get-tuple-element.47.row_ref) | copy-start | bytes 100
  10.3 12.0 %copy-start.18 = (s32[4]{0:T(128)S(1)}, s32[4]{0:T(128)}, u32[]{:S(2)}) copy-start(s32[4]{0:T(128)} %param.23) | copy-start | bytes 52
  10.3 17.2 %copy-start = (bf16[8192,128]{1,0:T(8,128)(2,1)S(1)}, bf16[8192,128]{1,0:T(8,128)(2,1)}, u32[]{:S(2)}) copy-start(bf16[8192,128]{1,0:T(8,128)(2,1)} %refs_3_.1) | copy-start | bytes 6291460
  16.3 49.3 %all-to-all-start = ((bf16[8,64,2688]{2,1,0:T(8,128)(2,1)}), bf16[8,64,2688]{2,1,0:T(8,128)(2,1)}, u32[]{:S(2)}, u32[]{:S(2)}) async-start(bf16[8,64,2688]{2,1,0:T(8,128)(2,1)} %serve.1), calls=%async_computation | async-start | bytes 5505024 | tf_op jit(solution)/shard_map/all_to_all | solution.py:942
  22.3 194.9 %reduce-scatter.2.cloned.1.call-start = ((), (), s32[]{:S(2)}) async-start(), calls=%async_computation.3 | async-start | bytes 3538944 | tf_op jit(solution)/shard_map/reduce_scatter | solution.py:958
  27.6 5.4 %copy-start.8 = (bf16[8192,256]{1,0:T(8,128)(2,1)S(1)}, bf16[8192,256]{1,0:T(8,128)(2,1)}, u32[]{:S(2)}) copy-start(bf16[8192,256]{1,0:T(8,128)(2,1)} %refs_1_.3) | copy-start | bytes 12582916
  92.6 16.7 %copy-start.10 = (bf16[384,256]{1,0:T(8,128)(2,1)S(1)}, bf16[384,256]{1,0:T(8,128)(2,1)}, u32[]{:S(2)}) copy-start(bf16[384,256]{1,0:T(8,128)(2,1)} %get-tuple-element.29.q_ref) | copy-start | bytes 589828
  109.4 1.4 copy-start.12
  110.8 2.2 copy-start.7
  112.3 20.2 %copy-start.3 = (bf16[384,256]{1,0:T(8,128)(2,1)}, bf16[384,256]{1,0:T(8,128)(2,1)S(1)}, u32[]{:S(2)}) copy-start(bf16[384,256]{1,0:T(8,128)(2,1)S(1)} %get-tuple-element.31.refs_0_.o_ref.attn) | copy-start | bytes 589828
  113.0 13.5 %copy-start.17 = (f32[384,256]{1,0:T(8,128)S(1)}, f32[384,256]{1,0:T(8,128)}, u32[]{:S(2)}) copy-start(f32[384,256]{1,0:T(8,128)} %get-tuple-element.33) | copy-start | bytes 1179652
  126.5 6.0 %copy-start.1 = (f32[384,128]{1,0:T(8,128)S(1)}, f32[384,128]{1,0:T(8,128)}, u32[]{:S(2)}) copy-start(f32[384,128]{1,0:T(8,128)} %get-tuple-element.49.stab) | copy-start | bytes 589828
  126.5 6.0 %copy-start.2 = (f32[384,128]{1,0:T(8,128)S(1)}, f32[384,128]{1,0:T(8,128)}, u32[]{:S(2)}) copy-start(f32[384,128]{1,0:T(8,128)} %get-tuple-element.50.ctab) | copy-start | bytes 589828
  126.5 6.0 %copy-start.13 = (bf16[2,8,384,128]{3,2,1,0:T(8,128)(2,1)S(1)}, bf16[2,8,384,128]{3,2,1,0:T(8,128)(2,1)}, u32[]{:S(2)}) copy-start(bf16[2,8,384,128]{3,2,1,0:T(8,128)(2,1)} %gather_kv.1.kv_ref) | copy-start | bytes 4718596
  135.2 0.7 copy-start.4
  135.9 1.1 copy-start.11
  192.6 24.6 %copy-start.14 = (f32[384,512]{1,0:T(8,128)S(1)}, f32[384,512]{1,0:T(8,128)}, u32[]{:S(2)}) copy-start(f32[384,512]{1,0:T(8,128)} %get-tuple-element.36) | copy-start | bytes 2359300
  192.6 26.4 %copy-start.5 = (bf16[384,256]{1,0:T(8,128)(2,1)S(1)}, bf16[384,256]{1,0:T(8,128)(2,1)}, u32[]{:S(2)}) copy-start(bf16[384,256]{1,0:T(8,128)(2,1)} %copy-done.4) | copy-start | bytes 589828
  192.6 26.4 %copy-start.6 = (bf16[384,128]{1,0:T(8,128)(2,1)S(1)}, bf16[384,128]{1,0:T(8,128)(2,1)}, u32[]{:S(2)}) copy-start(bf16[384,128]{1,0:T(8,128)(2,1)} %scatter_kv.1.grad_kv.refs_2_) | copy-start | bytes 294916
  192.6 75.8 %all-to-all-start.1 = ((bf16[8,64,2688]{2,1,0:T(8,128)(2,1)}), bf16[8,64,2688]{2,1,0:T(8,128)(2,1)}, u32[]{:S(2)}, u32[]{:S(2)}) async-start(bf16[8,64,2688]{2,1,0:T(8,128)(2,1)} %get-tuple-element.41), calls=%async_computation.2 | async-start | bytes 5505024 | tf_op jit(solution)/shard_map/all_to_all | solution.py:997
  219.0 2.2 copy-start.9
  221.2 46.4 %copy-start.15 = (f32[384,512]{1,0:T(8,128)S(1)}, f32[384,512]{1,0:T(8,128)}, u32[]{:S(2)}) copy-start(f32[384,512]{1,0:T(8,128)} %get-tuple-element.40) | copy-start | bytes 2359300
Sparse Core Ops, SparseCore 0:
  11.1 79.7 all-gather.1
Sparse Core Ops, SparseCore 1:
  126.5 90.5 reduce-scatter.1
